TPU v7x, 128 devices: a whole 4x4x4 slice. The times are simulated.
128 devices in a mesh: rep: 4 (over y_hi, core), fsdp: 32 (over x, z, y_lo).
Axes of the slice: x: 4, y: 4 (y_hi: 2, y_lo: 2; y = y_hi * 2 + y_lo), z: 4, core: 2. Of those that a mesh axis runs over, the one named last changes fastest.
Arguments:
- tokens: bfloat16 [131072, 8192], P(('rep', 'fsdp')), may hold values from -24 to 24
- cotangent: bfloat16 [131072, 512], P(('rep', 'fsdp')), may hold values from -0.015625 to 0.015625
- old_weight: bfloat16 [8192, 512], P(('rep', 'fsdp')), may hold values from -0.0625 to 0.0625
- old_first: float32 [8192, 512], P(('rep', 'fsdp')), may hold values from -4 to 4
- old_second: float32 [8192, 512], P(('rep', 'fsdp')), may hold values from 0.05 to 2
- old_owner: int32 [128], replicated, may hold values from 0 to 127, each once
- new_owner: int32 [32], replicated, may hold values from 0 to 31, each once
Outputs:
- projected: bfloat16 [131072, 512], P(('rep', 'fsdp'))
- new_weight: bfloat16 [8192, 512], P(('rep', 'fsdp'))
- new_first: float32 [8192, 512], P(('rep', 'fsdp'))
- new_second: float32 [8192, 512], P(('rep', 'fsdp'))
Inputs may be any that keep to these rules, and one draw needn't show every extreme that they name: `old_owner`: a permutation. `new_owner`: a permutation.
All inputs are finite; a program needn't handle non-finite values.
Results may differ from a plain program's by a relative error of at most 0.008.
Values may be sent and summed in bfloat16 or wider, within the bound.
A program may use at most 192 MiB of HBM per device.

v0:
```python
import jax
import jax.numpy as jnp
from jax import lax
from jax.sharding import PartitionSpec as P

beta_one = 0.9
beta_two = 0.95
learn_rate = 0.001
decay_rate = 0.1
epsilon = 1e-08
correction_one = 1.0 - 0.9**10
correction_two = 1.0 - 0.95**10


def body(tokens, cotangent, old_weight, old_first, old_second, old_owner, new_owner):
    devices = lax.axis_size(("rep", "fsdp"))
    groups = lax.axis_size("rep")
    shards = lax.axis_size("fsdp")
    tok_rows = tokens.shape[0]
    feature_count = tokens.shape[1]
    out_width = cotangent.shape[1]
    row_block = old_weight.shape[0]
    group_block = row_block * groups
    strip = row_block * out_width // devices
    slot_ids = jnp.arange(devices, dtype=jnp.int32)
    placing = jnp.take(new_owner, slot_ids % shards) * groups + slot_ids // shards
    inverse = jnp.zeros((devices,), jnp.int32).at[old_owner].set(slot_ids)
    tok_order = jnp.take(tokens.reshape(tok_rows, shards, group_block), new_owner, axis=1).reshape(
        tok_rows, feature_count
    )

    def outgoing(source):
        return jnp.take(source.astype(jnp.float32).reshape(devices, strip), placing, axis=0)

    stacked = jnp.stack([outgoing(old_first), outgoing(old_second), outgoing(old_weight)])
    layers = stacked.shape[0]
    arrived = lax.all_to_all(stacked, ("rep", "fsdp"), split_axis=1, concat_axis=1, tiled=True)
    moved = jnp.take(arrived, inverse, axis=1).reshape(layers, row_block, out_width)
    first_rows = moved[0]
    second_rows = moved[1]
    weight_rows = moved[2].astype(jnp.bfloat16)
    group_weight = lax.all_gather(weight_rows, "rep", axis=0, tiled=True)
    outputs = jnp.dot(
        tok_order,
        lax.all_gather(group_weight, "fsdp", axis=0, tiled=True),
        preferred_element_type=jnp.float32,
    )
    projected = outputs.astype(jnp.bfloat16)
    partial_sum = lax.psum_scatter(
        lax.dot_general(
            tok_order, cotangent, (((0,), (0,)), ((), ())), preferred_element_type=jnp.float32
        ).astype(jnp.bfloat16),
        "fsdp",
        scatter_dimension=0,
        tiled=True,
    )
    gradient = lax.psum_scatter(partial_sum, "rep", scatter_dimension=0, tiled=True).astype(
        jnp.float32
    )
    first_next = beta_one * first_rows + (1.0 - beta_one) * gradient
    second_next = beta_two * second_rows + (1.0 - beta_two) * gradient * gradient
    step_size = first_next / correction_one / (jnp.sqrt(second_next / correction_two) + epsilon)
    updated = (
        weight_rows.astype(jnp.float32) * (1.0 - learn_rate * decay_rate) - learn_rate * step_size
    ).astype(jnp.bfloat16)
    return (projected, updated, first_next, second_next)


def solution(mesh):
    placed = (
        P(("rep", "fsdp"), None),
        P(("rep", "fsdp"), None),
        P(("rep", "fsdp"), None),
        P(("rep", "fsdp"), None),
        P(("rep", "fsdp"), None),
        P(),
        P(),
    )
    return jax.shard_map(
        body,
        mesh=mesh,
        in_specs=placed,
        out_specs=(
            P(("rep", "fsdp"), None),
            P(("rep", "fsdp"), None),
            P(("rep", "fsdp"), None),
            P(("rep", "fsdp"), None),
        ),
        check_vma=False,
    )
```

profile of v0, /device:TPU:1, one launch (start us, length us, event | category | flops | bytes accessed | tf_op | source)
XLA Modules:
  0.0 545.8 jit_solution(16596674296264912171)
XLA Ops:
  7.2 0.0 reduce-scatter.3.cloned.1.call-start
  7.2 0.7 compare_select_fusion.5
  8.0 0.7 compare_and_fusion.2
  8.6 22.4 %copy.16 = bf16[1024,8192]{0,1:T(8,128)(2,1)} copy(bf16[1024,8192]{1,0:T(8,128)(2,1)} %param.9) | data formatting | bytes 33554432 | tf_op args[0]
  31.0 22.6 %copy.17 = bf16[1024,32,256]{2,0,1:T(8,128)(2,1)} copy(bf16[1024,32,256]{0,2,1:T(8,128)(2,1)} %bitcast.19) | data formatting | bytes 33554432 | tf_op jit(solution)/shard_map/reshape | solution.py:28
  53.6 13.0 %gather_fusion = bf16[32,1024,256]{2,1,0:T(8,128)(2,1)} fusion(bf16[1024,32,256]{2,0,1:T(8,128)(2,1)} %copy.17, s32[1024]{0:T(1024)S(1)} %pad_clamp_fusion.3), kind=kCustom, calls=%fused_computation.3 | custom fusion | bytes 33554560 | tf_op jit(solution)/shard_map/jit(_take)/gather | solution.py:28
  66.6 22.5 %copy.18 = bf16[1024,32,256]{0,2,1:T(8,128)(2,1)} copy(bf16[1024,32,256]{2,0,1:T(8,128)(2,1)} %bitcast.18) | data formatting | bytes 33554432 | tf_op jit(solution)/shard_map/jit(_take)/gather | solution.py:28
  89.1 0.1 broadcast_in_dim.46
  89.2 14.2 %bitcast_select_fusion = bf16[1024,8192]{0,1:T(8,128)(2,1)} fusion(bf16[1024,32,256]{0,2,1:T(8,128)(2,1)} %copy.18, pred[8192]{0:T(1024)(128)(4,1)S(1)} %broadcast_in_dim.47), kind=kLoop, calls=%fused_computation.7 | loop fusion | flops 8388608 | bytes 33562624 | tf_op jit(solution)/shard_map/jit(_take)/select_n | solution.py:28
  103.4 17.0 %convolution_convert_fusion = bf16[8192,512]{1,0:T(8,128)(2,1)} fusion(bf16[1024,8192]{0,1:T(8,128)(2,1)} %bitcast_select_fusion, bf16[1024,512]{1,0:T(8,128)(2,1)S(1)} %copy-done), kind=kOutput, calls=%fused_computation.8 | convolution fusion | flops 8594128896 | bytes 26214400 | tf_op jit(solution)/shard_map/dot_general | solution.py:50
  120.5 1.2 gather_fusion.1
  121.8 0.8 gather_fusion.3
  122.6 0.8 gather_fusion.4
  123.4 0.8 gather_fusion.5
  124.2 0.1 select_bitcast_fusion.3
  124.3 1.1 copy.19
  125.4 11.5 %all-to-all-start = ((f32[3,128,256]{2,0,1:T(4,128)}), f32[3,128,256]{2,0,1:T(4,128)S(1)}, u32[]{:S(2)}, u32[]{:S(2)}) async-start(f32[3,128,256]{2,0,1:T(4,128)} %copy.19), calls=%async_computation | async-start | bytes 1048576 | tf_op jit(solution)/shard_map/all_to_all | solution.py:37
  136.9 0.0 all-gather.2.cloned.1.call-start
  136.9 1.0 scatter_custom_fusion
  138.0 13.6 %all-to-all-done = f32[3,128,256]{2,0,1:T(4,128)S(1)} async-done(((f32[3,128,256]{2,0,1:T(4,128)}), f32[3,128,256]{2,0,1:T(4,128)S(1)}, u32[]{:S(2)}, u32[]{:S(2)}) %all-to-all-start) | async-done | bytes 393248 | tf_op jit(solution)/shard_map/all_to_all | solution.py:37
  151.5 0.9 gather_fusion.2
  152.4 0.2 select_bitcast_fusion
  152.6 0.4 fusion.4
  153.0 12.1 %all_gather.6 = bf16[256,512]{1,0:T(8,128)(2,1)} all-gather(bf16[64,512]{1,0:T(8,128)(2,1)S(1)} %convert_element_type.20), channel_id=1, replica_groups=mesh['rep'=4,'fsdp'=32] {'rep'}, dimensions={0}, use_global_device_ids=true | all-gather | bytes 327680 | tf_op jit(solution)/shard_map/all_gather | solution.py:42
  165.1 0.0 all-gather.2.cloned.1.call-update
  165.1 0.2 reduce-scatter.5.cloned.1.call-start
  165.4 0.8 fusion.3
  166.2 151.7 %reduce-scatter.3.cloned.1.call-done = bf16[256,512]{1,0:T(8,128)(2,1)} async-done(((bf16[8192,512]{1,0:T(8,128)(2,1)}), bf16[256,512]{1,0:T(8,128)(2,1)}) %reduce-scatter.3.cloned.1.call-update) | async-done | bytes 262160 | tf_op jit(solution)/shard_map/reduce_scatter | solution.py:49
  318.0 189.4 %all-gather.2.cloned.1.call-done = bf16[8192,512]{1,0:T(8,128)(2,1)} async-done(((bf16[256,512]{1,0:T(8,128)(2,1)}), bf16[8192,512]{1,0:T(8,128)(2,1)}) %all-gather.2.cloned.1.call-update) | async-done | bytes 8388624 | tf_op jit(solution)/shard_map/all_gather | solution.py:45
  507.4 15.6 %convolution_convert_fusion.1 = bf16[1024,512]{1,0:T(8,128)(2,1)} fusion(bf16[1024,8192]{0,1:T(8,128)(2,1)} %bitcast_select_fusion, bf16[8192,512]{1,0:T(8,128)(2,1)} %all-gather.2.cloned.1.call-done), kind=kOutput, calls=%fused_computation.9 | convolution fusion | flops 8590458880 | bytes 26214400 | tf_op jit(solution)/shard_map/dot_general | solution.py:43
  522.9 14.7 %reduce-scatter.5.cloned.1.call-done = bf16[64,512]{1,0:T(8,128)(2,1)} async-done(((bf16[256,512]{1,0:T(8,128)(2,1)}), bf16[64,512]{1,0:T(8,128)(2,1)}) %reduce-scatter.5.cloned.1.call-update) | async-done | bytes 65552 | tf_op jit(solution)/shard_map/reduce_scatter | solution.py:57
  537.6 1.6 subtract_convert_fusion
  (32 shorter events, 0.3 us)
Async XLA Ops:
  7.2 96.2 %copy-start = (bf16[1024,512]{1,0:T(8,128)(2,1)S(1)}, bf16[1024,512]{1,0:T(8,128)(2,1)}, u32[]{:S(2)}) copy-start(bf16[1024,512]{1,0:T(8,128)(2,1)} %param.10) | copy-start | bytes 3145732
  7.2 310.8 %reduce-scatter.3.cloned.1.call-start = ((), (), s32[]{:S(2)}) async-start(), calls=%async_computation.4 | async-start | bytes 8650752 | tf_op jit(solution)/shard_map/reduce_scatter | solution.py:49
  103.4 17.1 %copy-start.2 = (f32[64,512]{1,0:T(8,128)S(1)}, f32[64,512]{1,0:T(8,128)}, u32[]{:S(2)}) copy-start(f32[64,512]{1,0:T(8,128)} %param.12) | copy-start | bytes 393220
  103.4 17.2 %copy-start.1 = (s32[32]{0:T(128)S(1)}, s32[32]{0:T(128)}, u32[]{:S(2)}) copy-start(s32[32]{0:T(128)} %param.15) | copy-start | bytes 388
  103.4 18.4 %copy-start.3 = (f32[64,512]{1,0:T(8,128)S(1)}, f32[64,512]{1,0:T(8,128)}, u32[]{:S(2)}) copy-start(f32[64,512]{1,0:T(8,128)} %param.13) | copy-start | bytes 393220
  103.4 20.0 %copy-start.4 = (bf16[64,512]{1,0:T(8,128)(2,1)S(1)}, bf16[64,512]{1,0:T(8,128)(2,1)}, u32[]{:S(2)}) copy-start(bf16[64,512]{1,0:T(8,128)(2,1)} %param.11) | copy-start | bytes 196612
  103.4 33.5 %copy-start.5 = (s32[128]{0:T(128)S(1)}, s32[128]{0:T(128)}, u32[]{:S(2)}) copy-start(s32[128]{0:T(128)} %param.14) | copy-start | bytes 1540
  125.4 26.2 %all-to-all-start = ((f32[3,128,256]{2,0,1:T(4,128)}), f32[3,128,256]{2,0,1:T(4,128)S(1)}, u32[]{:S(2)}, u32[]{:S(2)}) async-start(f32[3,128,256]{2,0,1:T(4,128)} %copy.19), calls=%async_computation | async-start | bytes 1048576 | tf_op jit(solution)/shard_map/all_to_all | solution.py:37
  136.9 370.5 %all-gather.2.cloned.1.call-start = ((), (), s32[]{:S(2)}) async-start(), calls=%async_computation.3 | async-start | bytes 8650752 | tf_op jit(solution)/shard_map/all_gather | solution.py:45
  165.1 372.5 %reduce-scatter.5.cloned.1.call-start = ((), (), s32[]{:S(2)}) async-start(), calls=%async_computation.5 | async-start | bytes 327680 | tf_op jit(solution)/shard_map/reduce_scatter | solution.py:57
Sparse Core Ops, SparseCore 0:
  120.6 197.3 reduce-scatter.2
  319.6 187.7 all-gather.1
  509.9 27.6 reduce-scatter.4
where the time goes:
time: 548 us; the launch traced here: 546 us
  waiting for transfers between devices  369 us (67%)
  local copies, waits for them, and re-layouts  87.6 us (16%)
  matrix products  32.6 us (6%)
  other arithmetic  18.3 us (3%)
  between operations  14 us (3%)
  blocking collectives  12.1 us (2%)
  starting transfers between devices  11.8 us (2%)
    all_gather x1, waiting for transfers between devices, body(): lax.all_gather(group_weight, 'fsdp', axis=0, tiled=True)  189 us
    reduce_scatter x1, waiting for transfers between devices, body(): lax.psum_scatter(lax.dot_general(tok_order, cotangent, (((0,), (0,)), (()...  152 us
    gather x2, local copies, waits for them, and re-layouts, body(): jnp.take(tokens.reshape(tok_rows, shards, group_block), new_owner, axis=1)  35.5 us
    reshape x1, local copies, waits for them, and re-layouts, body(): tokens.reshape(tok_rows, shards, group_block)  22.6 us
    unnamed x13, local copies, waits for them, and re-layouts  22.4 us
    dot_general x1, matrix products, body(): lax.dot_general(tok_order, cotangent, (((0,), (0,)), ((), ())), preferred...  17 us
    dot_general x1, matrix products, body(): jnp.dot(tok_order, lax.all_gather(group_weight, 'fsdp', axis=0, tiled=Tru...  15.6 us
    select_n x2, other arithmetic, body(): jnp.take(tokens.reshape(tok_rows, shards, group_block), new_owner, axis=1)  14.9 us
  transfers between devices with their start and end apart: 4, of which 4 were waited for; matrix products, arithmetic and copies ran while one was open for 4% of the time, Pallas kernels for 0%

commit v1 on v0

v1 whole, which is shorter than its diff:
```python
import functools
import jax
import jax.numpy as jnp
from jax import lax
from jax.experimental import pallas as pl
from jax.experimental.pallas import tpu as pltpu
from jax.sharding import PartitionSpec as P

beta_one = 0.9
beta_two = 0.95
learn_rate = 0.001
decay_rate = 0.1
epsilon = 1e-08
correction_one = 1.0 - 0.9**10
correction_two = 1.0 - 0.95**10

MESH = pl.DeviceIdType.MESH
F32 = jnp.float32
BF16 = jnp.bfloat16
ROWS = 1024
D = 8192
KV = 512

RS_COLORS = (
    (("x", "y", "z"), (0, 48), (0, 256)),
    (("y", "z", "x"), (0, 48), (256, 256)),
    (("z", "x", "y"), (48, 16), (0, 512)),
)
AG_COLORS = (
    (("z", "y", "x"), (0, 48)),
    (("x", "z", "y"), (48, 48)),
    (("y", "x", "z"), (96, 32)),
)


def cut(spec):
    starts, sizes = [], []
    for axis in ("x", "z", "y"):
        kind, value = spec[axis]
        if axis == "y":
            if kind == "at":
                starts += [lax.rem(value, 2), value // 2]
                sizes += [1, 1]
            elif kind == "half":
                starts += [value, 0]
                sizes += [1, 2]
            else:
                starts += [0, 0]
                sizes += [2, 2]
        else:
            if kind == "at":
                starts.append(value)
                sizes.append(1)
            elif kind == "half":
                starts.append(2 * value)
                sizes.append(2)
            else:
                starts.append(0)
                sizes.append(4)
    return starts, sizes


ALL = ("all", 0)


class View:
    def __init__(self, ref, spec, rows, cols):
        self.ref, self.rows, self.cols = ref, rows, cols
        self.starts, self.sizes = cut(spec)

    @property
    def at(self):
        lead = tuple(pl.ds(s, n) for s, n in zip(self.starts, self.sizes))
        return self.ref.at[lead + (pl.ds(*self.rows), pl.ds(*self.cols))]

    def index(self, i):
        return tuple(s + k for s, k in zip(self.starts, i)) + (
            pl.ds(*self.rows),
            pl.ds(*self.cols),
        )


def own(ref, sizes, rows, cols, offset=(0, 0, 0, 0)):
    v = View.__new__(View)
    v.ref, v.rows, v.cols = ref, (0, rows), (0, cols)
    v.starts, v.sizes = list(offset), list(sizes)
    return v


def add_views(dst, sources, dtype):
    sizes = dst.sizes
    count = sizes[0] * sizes[1] * sizes[2] * sizes[3]

    def step(n, carry):
        i3 = lax.rem(n, sizes[3])
        n = n // sizes[3]
        i2 = lax.rem(n, sizes[2])
        n = n // sizes[2]
        i1 = lax.rem(n, sizes[1])
        i0 = n // sizes[1]
        i = (i0, i1, i2, i3)
        total = sources[0].ref[sources[0].index(i)].astype(F32)
        for s in sources[1:]:
            total = total + s.ref[s.index(i)].astype(F32)
        dst.ref[dst.index(i)] = total.astype(dtype)
        return carry

    lax.fori_loop(0, count, step, 0)


def kernel(
    nown_ref, place_ref, tok_hbm, cot_ref, w_ref,
    out_ref, grad_ref,
    tok, G, W, part, recv, S, perm,
    ra0, rb0, sa0, sb0, t30, t40,
    ra1, rb1, sa1, sb1, t31, t41,
    ra2, rb2, sa2, sb2, t32, t42,
    tok_sem, own_sem,
    ag_s, ag_r, die_s, die_r, ex_s, ex_r, rs_s, rs_r,
):
    r = lax.axis_index("rep")
    f = lax.axis_index("fsdp")
    yh, core = r // 2, lax.rem(r, 2)
    x, z, yl = f // 8, lax.rem(f // 2, 4), lax.rem(f, 2)
    me = {"x": x, "y": yh * 2 + yl, "z": z, "c": core}
    landing = ((ra0, rb0, sa0, sb0, t30, t40), (ra1, rb1, sa1, sb1, t31, t41), (ra2, rb2, sa2, sb2, t32, t42))

    def device(**moved):
        p = dict(me, **moved)
        return ((p["y"] // 2) * 2 + p["c"], p["x"] * 8 + p["z"] * 2 + lax.rem(p["y"], 2))

    def ring(axis, d):
        return lax.rem(me[axis] + d, 4)

    def send(src, dst, ss, rs, to):
        return pltpu.make_async_remote_copy(
            src_ref=src, dst_ref=dst, send_sem=ss, recv_sem=rs, device_id=to, device_id_type=MESH
        )

    tok_copies = [
        pltpu.make_async_copy(
            tok_hbm.at[:, pl.ds(256 * q, 256)], tok.at[q], tok_sem.at[q]
        )
        for q in range(32)
    ]
    own_copy = pltpu.make_async_copy(w_ref, G.at[x, z, yl, yh, core], own_sem)
    own_copy.start()
    for c in tok_copies:
        c.start()

    barrier = pltpu.get_barrier_semaphore()
    for axis in ("x", "y", "z"):
        for d in (1, 2, 3):
            pl.semaphore_signal(barrier, inc=1, device_id=device(**{axis: ring(axis, d)}), device_id_type=MESH)
    partner = device(c=1 - core)
    pl.semaphore_signal(barrier, inc=1, device_id=partner, device_id_type=MESH)
    rho = lax.broadcasted_iota(jnp.int32, (256, 256), 0)
    kap = lax.broadcasted_iota(jnp.int32, (256, 256), 1)
    perm[...] = (kap == lax.rem(rho, 16) * 16 + rho // 16).astype(F32).astype(BF16)
    pl.semaphore_wait(barrier, 10)
    own_copy.wait()

    def gbox(spec, blocks):
        starts, sizes = cut(spec)
        lead = tuple(pl.ds(s, n) for s, n in zip(starts, sizes))
        return G.at[lead + (pl.ds(core, 1), pl.ds(*blocks), slice(None))]

    def ag_line(k):
        axes, blocks = AG_COLORS[k]
        a = axes[0]
        box = gbox({t: ("at", me[t]) for t in axes}, blocks)
        return [
            send(box, box, ag_s.at[k, d - 1], ag_r.at[k, d - 1], device(**{a: ring(a, d)}))
            for d in (1, 2, 3)
        ]

    def ag_plane(k):
        axes, blocks = AG_COLORS[k]
        a = axes[1]
        box = gbox({axes[0]: ALL, a: ("at", me[a]), axes[2]: ("at", me[axes[2]])}, blocks)
        return [
            send(box, box, ag_s.at[k, 2 + d], ag_r.at[k, 2 + d], device(**{a: ring(a, d)}))
            for d in (1, 2, 3)
        ]

    def ag_box(k, at, half=None):
        axes, blocks = AG_COLORS[k]
        first = ALL if half is None else ("half", half)
        return gbox({axes[0]: first, axes[1]: ALL, axes[2]: ("at", at)}, blocks)

    def ag_far(k):
        a = AG_COLORS[k][0][2]
        box = ag_box(k, me[a])
        return [
            send(box, box, ag_s.at[k, 6 + i], ag_r.at[k, 6 + i], device(**{a: ring(a, d)}))
            for i, d in enumerate((1, 3))
        ]

    def ag_relay(k):
        a = AG_COLORS[k][0][2]
        up = ag_box(k, ring(a, 3), 0)
        down = ag_box(k, ring(a, 1), 1)
        return [
            send(up, up, ag_s.at[k, 8], ag_r.at[k, 8], device(**{a: ring(a, 1)})),
            send(down, down, ag_s.at[k, 9], ag_r.at[k, 9], device(**{a: ring(a, 3)})),
        ]

    def die(k, d):
        a = AG_COLORS[k][0][2]
        box = ag_box(k, ring(a, d))
        return send(box, box, die_s.at[k, d], die_r.at[k, d], partner)

    def start(copies):
        for c in copies:
            c.start()

    def arrived(copies):
        for c in copies:
            c.wait_recv()

    colors = range(3)
    line = [c for k in colors for c in ag_line(k)]
    plane = [c for k in colors for c in ag_plane(k)]
    far = [c for k in colors for c in ag_far(k)]
    relay = [c for k in colors for c in ag_relay(k)]
    dies = [[die(k, d) for k in colors] for d in range(4)]

    start(line)
    arrived(line)
    start(plane)
    for c in tok_copies:
        c.wait()

    def grad_step(n, carry):
        g = n // 8
        m = lax.rem(n, 8)
        block = lax.dot_general(
            tok[nown_ref[n]], cot_ref[...], (((0,), (0,)), ((), ())), preferred_element_type=F32
        ).astype(BF16)
        for i in range(4):
            part[g, m // 2, lax.rem(m, 2), i // 2, i % 2] = block[64 * i : 64 * i + 64]
        return carry

    def exchange(g):
        return send(
            part.at[g, :, :, :, 1 - core], recv.at[g], ex_s.at[g], ex_r.at[g], partner
        )

    def gradient(lo, hi):
        lax.fori_loop(lo, hi, grad_step, 0)

    gradient(0, 4)
    arrived(plane)
    start(far)
    start(dies[0])
    gradient(4, 8)
    exchange(0).start()
    gradient(8, 16)
    exchange(1).start()
    gradient(16, 24)
    exchange(2).start()
    arrived(far)
    start(relay)
    start(dies[1])
    start(dies[3])
    gradient(24, 32)
    exchange(3).start()

    def chip_sum(g):
        exchange(g).wait_recv()

        def step(n, carry):
            i3 = lax.rem(n, 2)
            i2 = lax.rem(n // 2, 2)
            i1 = n // 4
            S[g, i1, i2, i3] = (
                part[g, i1, i2, i3, core].astype(F32) + recv[g, i1, i2, i3].astype(F32)
            ).astype(BF16)
            return carry

        lax.fori_loop(0, 16, step, 0)

    for g in range(4):
        chip_sum(g)

    def rs(k):
        (a1, a2, a3), rows, cols = RS_COLORS[k]
        la, lb, xa, xb, l3, l4 = landing[k]
        up, down = device(**{a1: ring(a1, 1)}), device(**{a1: ring(a1, 3)})

        def sv(p1, s2, s3=ALL):
            return View(S, {a1: ("at", p1), a2: s2, a3: s3}, rows, cols)

        h0, h1 = ("half", 0), ("half", 1)
        mine, nxt, prv, opp = me[a1], ring(a1, 1), ring(a1, 3), ring(a1, 2)
        hs = sv(opp, h0).sizes
        fs = sv(opp, ALL).sizes
        hoff = [0 if p == q else p for p, q in zip(hs, fs)]
        nr, nc = rows[1], cols[1]
        la_v, lb_v = own(la, hs, nr, nc), own(lb, hs, nr, nc)
        xa0, xa1 = own(xa, hs, nr, nc), own(xa, hs, nr, nc, hoff)
        xb0, xb1 = own(xb, hs, nr, nc), own(xb, hs, nr, nc, hoff)
        first = [
            send(sv(opp, h0).at, la_v.at, rs_s.at[k, 0], rs_r.at[k, 0], up),
            send(sv(opp, h1).at, lb_v.at, rs_s.at[k, 1], rs_r.at[k, 1], down),
            send(sv(nxt, h1).at, xa1.at, rs_s.at[k, 2], rs_r.at[k, 2], up),
            send(sv(prv, h0).at, xb0.at, rs_s.at[k, 3], rs_r.at[k, 3], down),
        ]
        second = [
            send(sv(nxt, h0).at, xa0.at, rs_s.at[k, 4], rs_r.at[k, 4], up),
            send(sv(prv, h1).at, xb1.at, rs_s.at[k, 5], rs_r.at[k, 5], down),
        ]

        def fold_first():
            add_views(sv(nxt, h0), [sv(nxt, h0), la_v], BF16)
            add_views(sv(prv, h1), [sv(prv, h1), lb_v], BF16)

        full = sv(mine, ALL)

        def fold_second():
            add_views(full, [full, own(xa, fs, nr, nc), own(xb, fs, nr, nc)], BF16)

        def uv(p2):
            return sv(mine, ("at", p2))

        us = uv(0).sizes
        l3_v = [own(l3.at[d], us, nr, nc) for d in range(3)]
        third = [
            send(uv(ring(a2, d)).at, l3_v[d - 1].at, rs_s.at[k, 5 + d], rs_r.at[k, 5 + d], device(**{a2: ring(a2, d)}))
            for d in (1, 2, 3)
        ]

        def fold_third():
            add_views(uv(me[a2]), [uv(me[a2])] + l3_v, BF16)

        def vv(p3):
            return sv(mine, ("at", me[a2]), ("at", p3))

        l4_v = [own(l4.at[d], [1, 1, 1, 1], nr, nc) for d in range(3)]
        fourth = [
            send(vv(ring(a3, d)).at, l4_v[d - 1].at, rs_s.at[k, 8 + d], rs_r.at[k, 8 + d], device(**{a3: ring(a3, d)}))
            for d in (1, 2, 3)
        ]

        def fold_fourth():
            zero = (0, 0, 0, 0)
            v = vv(me[a3])
            total = v.ref[v.index(zero)].astype(F32)
            for w in l4_v:
                total = total + w.ref[w.index(zero)].astype(F32)
            grad_ref[pl.ds(*rows), pl.ds(*cols)] = total

        return first, fold_first, second, fold_second, third, fold_third, fourth, fold_fourth

    plans = [rs(k) for k in colors]
    first = [c for p in plans for c in p[0]]
    second = [c for p in plans for c in p[2]]
    third = [c for p in plans for c in p[4]]
    fourth = [c for p in plans for c in p[6]]

    start(first)

    arrived(relay)
    start(dies[2])
    for d in (0, 1, 3, 2):
        arrived(dies[d])

    def place(s, b):
        return G[
            place_ref[s, 0], place_ref[s, 1], place_ref[s, 2], place_ref[s, 3], place_ref[s, 4],
            pl.ds(pl.multiple_of(b, 16), 16), :,
        ]

    def assemble(n, carry):
        b0 = (n // 4) * 16
        j0 = lax.rem(n, 4) * 16
        halves = [
            jnp.concatenate([place(2 * (j0 + t) + h, b0) for t in range(16)], axis=0)
            for h in range(2)
        ]
        got = jnp.dot(perm[...], jnp.concatenate(halves, axis=1), preferred_element_type=F32).astype(BF16)
        for b in range(16):
            W[pl.ds(pl.multiple_of((b0 + b) * 64 + j0, 16), 16), :] = got[16 * b : 16 * b + 16]
        return carry

    lax.fori_loop(0, 32, assemble, 0)

    for c in first[0:2] + first[4:6] + first[8:10]:
        c.wait_recv()
    for p in plans:
        p[1]()
    start(second)

    def project(m, carry):
        at = pl.multiple_of(m * 256, 256)
        rows = jnp.concatenate([tok[q, pl.ds(at, 256), :] for q in range(32)], axis=1)
        out_ref[pl.ds(at, 256), :] = jnp.dot(rows, W[...], preferred_element_type=F32).astype(BF16)
        return carry

    lax.fori_loop(0, 2, project, 0)
    for c in first[2:4] + first[6:8] + first[10:12] + second:
        c.wait_recv()
    for p in plans:
        p[3]()
    start(third)
    lax.fori_loop(2, 4, project, 0)
    arrived(third)
    for p in plans:
        p[5]()
    start(fourth)
    arrived(fourth)
    for p in plans:
        p[7]()

    for c in line + plane + far + relay + [c for d in dies for c in d]:
        c.wait_send()
    for g in range(4):
        exchange(g).wait_send()
    for c in first + second + third + fourth:
        c.wait_send()


def landing_shapes():
    shapes = []
    at = ("at", 0)
    for (a1, a2, a3), rows, cols in RS_COLORS:
        n, m = rows[1], cols[1]

        def size(spec):
            return tuple(static_sizes(spec))

        half = size({a1: "at", a2: "half", a3: "all"}) + (n, m)
        full = size({a1: "at", a2: "all", a3: "all"}) + (n, m)
        line = size({a1: "at", a2: "at", a3: "all"}) + (n, m)
        shapes += [
            pltpu.VMEM(half, BF16), pltpu.VMEM(half, BF16),
            pltpu.VMEM(full, BF16), pltpu.VMEM(full, BF16),
            pltpu.VMEM((3,) + line, BF16), pltpu.VMEM((3, 1, 1, 1, 1, n, m), BF16),
        ]
    return shapes


def static_sizes(spec):
    sizes = []
    for axis in ("x", "z", "y"):
        kind = spec[axis]
        if axis == "y":
            sizes += {"at": [1, 1], "half": [1, 2], "all": [2, 2]}[kind]
        else:
            sizes += {"at": [1], "half": [2], "all": [4]}[kind]
    return sizes


def fused(new_owner, places, tokens, cotangent, shard):
    smem = pl.BlockSpec(memory_space=pltpu.SMEM)
    vmem = pl.BlockSpec(memory_space=pltpu.VMEM)
    dma = pltpu.SemaphoreType.DMA
    return pl.pallas_call(
        kernel,
        out_shape=(
            jax.ShapeDtypeStruct((ROWS, KV), BF16),
            jax.ShapeDtypeStruct((64, KV), F32),
        ),
        in_specs=[smem, smem, pl.BlockSpec(memory_space=pl.ANY), vmem, vmem],
        out_specs=(vmem, vmem),
        scratch_shapes=[
            pltpu.VMEM((32, ROWS, 256), BF16),
            pltpu.VMEM((4, 4, 2, 2, 2, 128, 256), BF16),
            pltpu.VMEM((D, KV), BF16),
            pltpu.VMEM((4, 4, 2, 2, 2, 64, KV), BF16),
            pltpu.VMEM((4, 4, 2, 2, 64, KV), BF16),
            pltpu.VMEM((4, 4, 2, 2, 64, KV), BF16),
            pltpu.VMEM((256, 256), BF16),
        ]
        + landing_shapes()
        + [
            dma((32,)), dma,
            dma((3, 10)), dma((3, 10)), dma((3, 4)), dma((3, 4)),
            dma((4,)), dma((4,)), dma((3, 12)), dma((3, 12)),
        ],
        compiler_params=pltpu.CompilerParams(
            collective_id=0, has_side_effects=True, vmem_limit_bytes=67_000_000
        ),
        name="gather_grad_project",
    )(new_owner, places, tokens, cotangent, shard)


def body(tokens, cotangent, old_weight, old_first, old_second, old_owner, new_owner):
    devices, shards, groups, strip = 128, 32, 4, 256
    slot_ids = jnp.arange(devices, dtype=jnp.int32)
    inverse = jnp.sum(
        jnp.where(old_owner[None, :] == slot_ids[:, None], slot_ids[None, :], 0), axis=1
    ).astype(jnp.int32)
    r, f = inverse // shards, inverse % shards
    places = jnp.stack([f // 8, (f // 2) % 4, f % 2, r // 2, r % 2], axis=1)
    placing = (new_owner[None, :] * groups + jnp.arange(groups, dtype=jnp.int32)[:, None]).reshape(devices)

    shard = old_weight.reshape(devices, strip)
    stacked = jnp.concatenate(
        [old_first.reshape(devices, strip).astype(BF16), old_second.reshape(devices, strip).astype(BF16), shard],
        axis=1,
    )
    outgoing = jnp.take(stacked, placing, axis=0)
    arrived = lax.all_to_all(outgoing, ("rep", "fsdp"), split_axis=0, concat_axis=0, tiled=True)
    projected, gradient = fused(new_owner, places, tokens, cotangent, shard)
    moved = jnp.take(arrived, inverse, axis=0).astype(F32)
    first_rows = moved[:, :strip].reshape(64, KV)
    second_rows = moved[:, strip : 2 * strip].reshape(64, KV)
    weight_rows = moved[:, 2 * strip :].reshape(64, KV)

    first_next = beta_one * first_rows + (1.0 - beta_one) * gradient
    second_next = beta_two * second_rows + (1.0 - beta_two) * gradient * gradient
    step_size = first_next / correction_one / (jnp.sqrt(second_next / correction_two) + epsilon)
    updated = (weight_rows * (1.0 - learn_rate * decay_rate) - learn_rate * step_size).astype(BF16)
    return (projected, updated, first_next, second_next)


def solution(mesh):
    rows = P(("rep", "fsdp"), None)
    return jax.shard_map(
        body,
        mesh=mesh,
        in_specs=(rows, rows, rows, rows, rows, P(), P()),
        out_specs=(rows, rows, rows, rows),
        check_vma=False,
    )
```

time: 548 us -> 97.9 us (0.18)
  waiting for transfers between devices: 369 us -> 0.01 us
  local copies, waits for them, and re-layouts: 87.6 us -> 8.72 us
  Pallas kernels: 0 us -> 68.7 us
  matrix products: 32.6 us -> 0 us
  between operations: 14 us -> 0.81 us
  other arithmetic: 18.3 us -> 5.97 us
  blocking collectives: 12.1 us -> 0 us
    all_gather x1 -> x0, waiting for transfers between devices: 189 us -> none  [body(): lax.all_gather(group_weight, 'fsdp', axis=0, tiled=True)]
    reduce_scatter x2 -> x0, waiting for transfers between devices: 166 us -> none  [the longest x1 152 us: body(): lax.psum_scatter(lax.dot_general(tok_order, cotangent, (((0,), (0,)), (()...]
    pallas_call x0 -> x1, Pallas kernels: none -> 68.7 us  [fused(): pl.pallas_call(kernel, out_shape=(jax.ShapeDtypeStruct((ROWS, KV), BF16),...]
    gather x7 -> x2, local copies, waits for them, and re-layouts: 39.9 us -> 1.74 us  [the longest x1 0.87 us: body(): outgoing = jnp.take(stacked, placing, axis=0)]
    dot_general x2 -> x0, matrix products: 32.6 us -> none  [the longest x1 17 us: body(): lax.dot_general(tok_order, cotangent, (((0,), (0,)), ((), ())), preferred...]
    reshape x4 -> x1, local copies, waits for them, and re-layouts: 22.6 us -> 0.87 us  [body(): shard = old_weight.reshape(devices, strip)]
    unnamed x13 -> x6, local copies, waits for them, and re-layouts: 22.4 us -> 4.58 us
    select_n x6 -> x3, other arithmetic: 15.1 us -> 0.04 us  [the longest x1 0.03 us: body(): places = jnp.stack([f // 8, f // 2 % 4, f % 2, r // 2, r % 2], axis=1)]
  transfers between devices with their start and end apart: 4 -> 1, of which waited for: 4 -> 0; matrix products, arithmetic and copies ran while one was open for 4% -> 2% of each run, Pallas kernels for 0% -> 71%
where the time goes in v1:
time: 97.9 us; the launch traced here: 96.1 us
  Pallas kernels  68.7 us (70%)
  starting transfers between devices  11.9 us (12%)
  local copies, waits for them, and re-layouts  8.72 us (9%)
  other arithmetic  5.97 us (6%)
    pallas_call x1, Pallas kernels, fused(): pl.pallas_call(kernel, out_shape=(jax.ShapeDtypeStruct((ROWS, KV), BF16),...  68.7 us
    all_to_all x1, starting transfers between devices, body(): lax.all_to_all(outgoing, ('rep', 'fsdp'), split_axis=0, concat_axis=0, ti...  11.9 us
    unnamed x6, local copies, waits for them, and re-layouts  4.58 us
  transfers between devices with their start and end apart: 1, of which 0 were waited for; matrix products, arithmetic and copies ran while one was open for 2% of the time, Pallas kernels for 71%

profile of v1, /device:TPU:1, one launch (start us, length us, event | category | flops | bytes accessed | tf_op | source)
XLA Modules:
  0.0 96.1 jit_solution(15716508575047484578)
XLA Ops:
  0.6 0.7 broadcast_multiply_fusion
  1.3 0.1 add.132
  1.4 0.9 reshape.313.w_ref
  2.3 0.0 copy-start
  2.3 0.9 convert_element_type.20
  3.3 0.9 convert_element_type.18
  4.2 0.0 copy-done
  4.3 0.9 gather_fusion
  5.1 0.1 select_bitcast_fusion
  5.2 0.5 broadcast.463
  5.7 0.7 reduce
  6.5 0.7 reshape.336
  7.2 11.9 %all-to-all-start = ((bf16[128,2,384]{2,1,0:T(2,128)(2,1)}), bf16[128,2,384]{2,1,0:T(2,128)(2,1)}, u32[]{:S(2)}, u32[]{:S(2)}) async-start(bf16[128,2,384]{2,1,0:T(2,128)(2,1)} %reshape.336), calls=%async_computation | async-start | bytes 393216 | tf_op jit(solution)/shard_map/all_to_all | solution.py:504
  19.1 0.8 select_reduce_fusion
  19.9 0.7 copy.19.place_ref
  20.7 68.7 %gather_grad_project.1 = (bf16[1024,512]{1,0:T(8,128)(2,1)}, f32[64,512]{1,0:T(8,128)}) custom-call(s32[32]{0:T(128)} %nown_ref.1, s32[128,5]{1,0:T(8,128)} %copy.19.place_ref, bf16[1024,8192]{1,0:T(8,128)(2,1)} %tok_hbm.1, bf16[1024,512]{1,0:T(8,128)(2,1)} %cot_ref.1, bf16[128,256]{1,0:T(8,128)(2,1)} %copy-done), custom_call_target="tpu_custom_call" | custom-call | tf_op jit(solution)/shard_map/gather_grad_project/pallas_call | solution.py:458
  89.4 0.0 all-to-all-done
  89.4 1.6 %reshape.337 = bf16[128,1,768]{2,1,0:T(2,128)(2,1)S(1)} reshape(bf16[128,2,384]{2,1,0:T(2,128)(2,1)} %all-to-all-done) | data formatting | bytes 393216
  91.0 0.9 gather_fusion.1
  91.8 0.1 select_convert_fusion
  92.1 1.7 %subtract_convert_fusion = (bf16[64,512]{1,0:T(8,128)(2,1)}, f32[64,512]{1,0:T(8,128)}, f32[64,512]{1,0:T(8,128)}) fusion(f32[64,512]{1,0:T(8,128)S(1)} %mul.59, f32[64,512]{1,0:T(8,128)S(1)} %mul.62, f32[64,512]{1,0:T(8,128)} %get-tuple-element.8, f32[64,512]{1,0:T(8,128)S(1)} %mul.67), kind=kLoop, calls=%fused_computation.11 | loop fusion | flops 393216 | bytes 851968 | tf_op jit(solution)/shard_map/convert_element_type | solution.py:514
  93.8 2.3 %copy.26 = bf16[1024,512]{1,0:T(8,128)(2,1)} copy(bf16[1024,512]{1,0:T(8,128)(2,1)} %get-tuple-element.24) | data formatting | bytes 2097152
  (17 shorter events, 0.3 us)
Async XLA Ops:
  2.3 2.0 %copy-start = (bf16[128,256]{1,0:T(8,128)(2,1)}, bf16[128,256]{1,0:T(8,128)(2,1)S(1)}, u32[]{:S(2)}) copy-start(bf16[128,256]{1,0:T(8,128)(2,1)S(1)} %reshape.313.w_ref) | copy-start | bytes 196612
  7.2 82.2 %all-to-all-start = ((bf16[128,2,384]{2,1,0:T(2,128)(2,1)}), bf16[128,2,384]{2,1,0:T(2,128)(2,1)}, u32[]{:S(2)}, u32[]{:S(2)}) async-start(bf16[128,2,384]{2,1,0:T(2,128)(2,1)} %reshape.336), calls=%async_computation | async-start | bytes 393216 | tf_op jit(solution)/shard_map/all_to_all | solution.py:504

commit v2 on v1

--- a/solution.py
+++ b/solution.py
@@ -108,22 +108,32 @@
     lax.fori_loop(0, count, step, 0)
 
 
+def iota(shape, dim):
+    return lax.broadcasted_iota(jnp.int32, shape, dim)
+
+
+def one_hot(mask):
+    return mask.astype(F32).astype(BF16)
+
+
+def stack_halves(v):
+    return jnp.concatenate([v[:, :256], v[:, 256:]], axis=0)
+
+
 def kernel(
-    nown_ref, place_ref, tok_hbm, cot_ref, w_ref,
-    out_ref, grad_ref,
-    tok, G, W, part, recv, S, perm,
-    ra0, rb0, sa0, sb0, t30, t40,
-    ra1, rb1, sa1, sb1, t31, t41,
-    ra2, rb2, sa2, sb2, t32, t42,
-    tok_sem, own_sem,
-    ag_s, ag_r, die_s, die_r, ex_s, ex_r, rs_s, rs_r,
+    nown_ref, inv_ref, nown_vec, owner_vec, tok_hbm, cot_ref, w_ref, first_ref, second_ref,
+    out_ref, grad_ref, m_ref, wrow_ref,
+    tok, G, W, part, recv, S,
+    M0, C1, Y1, XZ, X1, Z1,
+    *rest,
 ):
+    (tok_sem, ag_s, ag_r, die_s, die_r, ex_s, ex_r, rs_s, rs_r, mv_s, mv_r) = rest[-11:]
+    landing = (rest[0:6], rest[6:12], rest[12:18])
     r = lax.axis_index("rep")
     f = lax.axis_index("fsdp")
     yh, core = r // 2, lax.rem(r, 2)
     x, z, yl = f // 8, lax.rem(f // 2, 4), lax.rem(f, 2)
     me = {"x": x, "y": yh * 2 + yl, "z": z, "c": core}
-    landing = ((ra0, rb0, sa0, sb0, t30, t40), (ra1, rb1, sa1, sb1, t31, t41), (ra2, rb2, sa2, sb2, t32, t42))
 
     def device(**moved):
         p = dict(me, **moved)
@@ -137,16 +147,19 @@
             src_ref=src, dst_ref=dst, send_sem=ss, recv_sem=rs, device_id=to, device_id_type=MESH
         )
 
-    tok_copies = [
-        pltpu.make_async_copy(
-            tok_hbm.at[:, pl.ds(256 * q, 256)], tok.at[q], tok_sem.at[q]
-        )
-        for q in range(32)
-    ]
-    own_copy = pltpu.make_async_copy(w_ref, G.at[x, z, yl, yh, core], own_sem)
-    own_copy.start()
-    for c in tok_copies:
-        c.start()
+    def start(copies):
+        for c in copies:
+            c.start()
+
+    def arrived(copies):
+        for c in copies:
+            c.wait_recv()
+
+    everything = []
+
+    def keep(copies):
+        everything.extend(copies)
+        return copies
 
     barrier = pltpu.get_barrier_semaphore()
     for axis in ("x", "y", "z"):
@@ -154,11 +167,30 @@
             pl.semaphore_signal(barrier, inc=1, device_id=device(**{axis: ring(axis, d)}), device_id_type=MESH)
     partner = device(c=1 - core)
     pl.semaphore_signal(barrier, inc=1, device_id=partner, device_id_type=MESH)
-    rho = lax.broadcasted_iota(jnp.int32, (256, 256), 0)
-    kap = lax.broadcasted_iota(jnp.int32, (256, 256), 1)
-    perm[...] = (kap == lax.rem(rho, 16) * 16 + rho // 16).astype(F32).astype(BF16)
-    pl.semaphore_wait(barrier, 10)
-    own_copy.wait()
+
+    tok_copies = [
+        pltpu.make_async_copy(tok_hbm.at[:, pl.ds(256 * q, 256)], tok.at[q], tok_sem.at[q])
+        for q in range(32)
+    ]
+    start(tok_copies)
+
+    sq = (128, 128)
+    split = one_hot(iota(sq, 1) == lax.rem(iota(sq, 0), 2) * 64 + iota(sq, 0) // 2)
+    G[x, z, yl, yh, core] = jnp.dot(split, stack_halves(w_ref[...]), preferred_element_type=F32).astype(BF16)
+
+    d = iota(sq, 1)
+    dc, dyl, dyh, dx, dz = d // 64, lax.rem(d // 32, 2), lax.rem(d // 16, 2), lax.rem(d // 4, 4), lax.rem(d, 4)
+    pick = one_hot((iota(sq, 0) == dx * 8 + dz * 2 + dyl)[:32])
+    block = 4.0 * jnp.dot(nown_vec[...].astype(F32).astype(BF16), pick, preferred_element_type=F32)
+    block = block + (dyh * 2 + dc)[:1].astype(F32)
+    sp = iota(sq, 0)
+    choose = one_hot(block == (2 * lax.rem(sp, 64) + sp // 64).astype(F32))
+    moments = jnp.concatenate(
+        [stack_halves(first_ref[...].astype(BF16)), stack_halves(second_ref[...].astype(BF16))], axis=1
+    )
+    moved = lax.dot_general(choose, moments, (((0,), (0,)), ((), ())), preferred_element_type=F32).astype(BF16)
+    for i in range(8):
+        M0[i // 4, (i // 2) % 2, i % 2] = moved[16 * i : 16 * i + 16]
 
     def gbox(spec, blocks):
         starts, sizes = cut(spec)
@@ -210,24 +242,40 @@
         box = ag_box(k, ring(a, d))
         return send(box, box, die_s.at[k, d], die_r.at[k, d], partner)
 
-    def start(copies):
-        for c in copies:
-            c.start()
-
-    def arrived(copies):
-        for c in copies:
-            c.wait_recv()
-
     colors = range(3)
-    line = [c for k in colors for c in ag_line(k)]
-    plane = [c for k in colors for c in ag_plane(k)]
-    far = [c for k in colors for c in ag_far(k)]
-    relay = [c for k in colors for c in ag_relay(k)]
-    dies = [[die(k, d) for k in colors] for d in range(4)]
-
+    line = keep([c for k in colors for c in ag_line(k)])
+    plane = keep([c for k in colors for c in ag_plane(k)])
+    far = keep([c for k in colors for c in ag_far(k)])
+    relay = keep([c for k in colors for c in ag_relay(k)])
+    dies = [keep([die(k, d) for k in colors]) for d in range(4)]
+
+    pl.semaphore_wait(barrier, 10)
     start(line)
+
+    mv_c = keep([send(M0.at[1 - core], C1.at[core], mv_s.at[0], mv_r.at[0], partner)])
+    start(mv_c)
+    C1[core] = M0[core]
+    mv_y = keep([
+        send(
+            C1.at[:, lax.rem(ring("y", d), 2), ring("y", d) // 2], Y1.at[yl, yh],
+            mv_s.at[d], mv_r.at[d], device(y=ring("y", d)),
+        )
+        for d in (1, 2, 3)
+    ])
+    mv_x = keep([
+        send(XZ.at[ring("x", d)], X1.at[x], mv_s.at[3 + d], mv_r.at[3 + d], device(x=ring("x", d)))
+        for d in (1, 2, 3)
+    ])
+    mv_z = keep([
+        send(X1.at[:, ring("z", d)], Z1.at[:, z], mv_s.at[6 + d], mv_r.at[6 + d], device(z=ring("z", d)))
+        for d in (1, 2, 3)
+    ])
+
     arrived(line)
     start(plane)
+    arrived(mv_c)
+    start(mv_y)
+    Y1[yl, yh] = C1[:, yl, yh]
     for c in tok_copies:
         c.wait()
 
@@ -241,33 +289,41 @@
             part[g, m // 2, lax.rem(m, 2), i // 2, i % 2] = block[64 * i : 64 * i + 64]
         return carry
 
-    def exchange(g):
-        return send(
-            part.at[g, :, :, :, 1 - core], recv.at[g], ex_s.at[g], ex_r.at[g], partner
-        )
+    exchange = keep([
+        send(part.at[g, :, :, :, 1 - core], recv.at[g], ex_s.at[g], ex_r.at[g], partner)
+        for g in range(4)
+    ])
 
     def gradient(lo, hi):
-        lax.fori_loop(lo, hi, grad_step, 0)
-
-    gradient(0, 4)
+        lax.fori_loop(lo, hi, grad_step, 0, unroll=4)
+
+    gradient(0, 8)
+    exchange[0].start()
     arrived(plane)
     start(far)
     start(dies[0])
-    gradient(4, 8)
-    exchange(0).start()
+    arrived(mv_y)
+    rows = Y1[...].reshape(128, 512)
+    swap = one_hot(iota(sq, 1) == lax.rem(iota(sq, 0), 8) * 16 + iota(sq, 0) // 8)
+    XZ[...] = jnp.dot(swap, rows, preferred_element_type=F32).astype(BF16).reshape(4, 4, 8, 512)
+    start(mv_x)
+    X1[x] = XZ[x]
     gradient(8, 16)
-    exchange(1).start()
+    exchange[1].start()
     gradient(16, 24)
-    exchange(2).start()
+    exchange[2].start()
+    arrived(mv_x)
+    start(mv_z)
+    Z1[:, z] = X1[:, z]
+    gradient(24, 32)
+    exchange[3].start()
     arrived(far)
     start(relay)
     start(dies[1])
     start(dies[3])
-    gradient(24, 32)
-    exchange(3).start()
 
     def chip_sum(g):
-        exchange(g).wait_recv()
+        exchange[g].wait_recv()
 
         def step(n, carry):
             i3 = lax.rem(n, 2)
@@ -353,70 +409,80 @@
         return first, fold_first, second, fold_second, third, fold_third, fourth, fold_fourth
 
     plans = [rs(k) for k in colors]
-    first = [c for p in plans for c in p[0]]
-    second = [c for p in plans for c in p[2]]
-    third = [c for p in plans for c in p[4]]
-    fourth = [c for p in plans for c in p[6]]
+    first = keep([c for p in plans for c in p[0]])
+    second = keep([c for p in plans for c in p[2]])
+    third = keep([c for p in plans for c in p[4]])
+    fourth = keep([c for p in plans for c in p[6]])
 
     start(first)
 
     arrived(relay)
     start(dies[2])
-    for d in (0, 1, 3, 2):
-        arrived(dies[d])
 
     def place(s, b):
+        i = inv_ref[s]
         return G[
-            place_ref[s, 0], place_ref[s, 1], place_ref[s, 2], place_ref[s, 3], place_ref[s, 4],
+            i // 32, lax.rem(i // 8, 4), lax.rem(i // 4, 2), lax.rem(i // 2, 2), lax.rem(i, 2),
             pl.ds(pl.multiple_of(b, 16), 16), :,
         ]
 
     def assemble(n, carry):
         b0 = (n // 4) * 16
         j0 = lax.rem(n, 4) * 16
-        halves = [
-            jnp.concatenate([place(2 * (j0 + t) + h, b0) for t in range(16)], axis=0)
-            for h in range(2)
-        ]
-        got = jnp.dot(perm[...], jnp.concatenate(halves, axis=1), preferred_element_type=F32).astype(BF16)
-        for b in range(16):
-            W[pl.ds(pl.multiple_of((b0 + b) * 64 + j0, 16), 16), :] = got[16 * b : 16 * b + 16]
+        for h in range(2):
+            got = jnp.swapaxes(jnp.stack([place(2 * (j0 + t) + h, b0) for t in range(16)], axis=0), 0, 1)
+            for b in range(16):
+                W[b0 + b, pl.ds(pl.multiple_of(j0, 16), 16), pl.ds(256 * h, 256)] = got[b]
         return carry
 
+    def project(m):
+        at = 256 * m
+        rows = jnp.concatenate([tok[q, pl.ds(at, 256), :] for q in range(32)], axis=1)
+        out_ref[pl.ds(at, 256), :] = jnp.dot(
+            rows, W[...].reshape(D, KV), preferred_element_type=F32
+        ).astype(BF16)
+
+    for d in (0, 1, 3, 2):
+        arrived(dies[d])
     lax.fori_loop(0, 32, assemble, 0)
-
-    for c in first[0:2] + first[4:6] + first[8:10]:
-        c.wait_recv()
     for p in plans:
+        arrived(p[0][:2])
         p[1]()
-    start(second)
-
-    def project(m, carry):
-        at = pl.multiple_of(m * 256, 256)
-        rows = jnp.concatenate([tok[q, pl.ds(at, 256), :] for q in range(32)], axis=1)
-        out_ref[pl.ds(at, 256), :] = jnp.dot(rows, W[...], preferred_element_type=F32).astype(BF16)
-        return carry
-
-    lax.fori_loop(0, 2, project, 0)
-    for c in first[2:4] + first[6:8] + first[10:12] + second:
-        c.wait_recv()
+        start(p[2])
+    project(0)
+    project(1)
     for p in plans:
+        arrived(p[0][2:] + p[2])
         p[3]()
-    start(third)
-    lax.fori_loop(2, 4, project, 0)
-    arrived(third)
+        start(p[4])
+    project(2)
+    project(3)
     for p in plans:
+        arrived(p[4])
         p[5]()
-    start(fourth)
-    arrived(fourth)
+        start(p[6])
+
+    arrived(mv_z)
+    owner = jnp.dot(
+        owner_vec[...].astype(F32).astype(BF16),
+        one_hot(iota(sq, 0) == lax.rem(iota(sq, 1), 4) * 32 + iota(sq, 1) // 4),
+        preferred_element_type=F32,
+    )
+    strips = Z1[...].reshape(128, 512)
+    halves = [
+        jnp.dot(
+            one_hot(owner == (2 * iota((64, 128), 0) + h).astype(F32)), strips, preferred_element_type=F32
+        ).astype(BF16)
+        for h in range(2)
+    ]
+    for i in range(2):
+        for h in range(2):
+            m_ref[i, :, pl.ds(256 * h, 256)] = halves[h][:, 256 * i : 256 * i + 256]
+    wrow_ref[...] = W[nown_ref[f] * 4 + r]
     for p in plans:
+        arrived(p[6])
         p[7]()
-
-    for c in line + plane + far + relay + [c for d in dies for c in d]:
-        c.wait_send()
-    for g in range(4):
-        exchange(g).wait_send()
-    for c in first + second + third + fourth:
+    for c in everything:
         c.wait_send()
 
 
@@ -451,7 +517,7 @@
     return sizes
 
 
-def fused(new_owner, places, tokens, cotangent, shard):
+def fused(new_owner, inverse, old_owner, tokens, cotangent, old_weight, old_first, old_second):
     smem = pl.BlockSpec(memory_space=pltpu.SMEM)
     vmem = pl.BlockSpec(memory_space=pltpu.VMEM)
     dma = pltpu.SemaphoreType.DMA
@@ -460,58 +526,55 @@
         out_shape=(
             jax.ShapeDtypeStruct((ROWS, KV), BF16),
             jax.ShapeDtypeStruct((64, KV), F32),
+            jax.ShapeDtypeStruct((2, 64, KV), BF16),
+            jax.ShapeDtypeStruct((64, KV), BF16),
         ),
-        in_specs=[smem, smem, pl.BlockSpec(memory_space=pl.ANY), vmem, vmem],
-        out_specs=(vmem, vmem),
+        in_specs=[smem, smem, vmem, vmem, pl.BlockSpec(memory_space=pl.ANY)] + [vmem] * 4,
+        out_specs=(vmem,) * 4,
         scratch_shapes=[
             pltpu.VMEM((32, ROWS, 256), BF16),
             pltpu.VMEM((4, 4, 2, 2, 2, 128, 256), BF16),
-            pltpu.VMEM((D, KV), BF16),
+            pltpu.VMEM((128, 64, KV), BF16),
             pltpu.VMEM((4, 4, 2, 2, 2, 64, KV), BF16),
             pltpu.VMEM((4, 4, 2, 2, 64, KV), BF16),
             pltpu.VMEM((4, 4, 2, 2, 64, KV), BF16),
-            pltpu.VMEM((256, 256), BF16),
+            pltpu.VMEM((2, 2, 2, 16, 512), BF16),
+            pltpu.VMEM((2, 2, 2, 16, 512), BF16),
+            pltpu.VMEM((2, 2, 2, 16, 512), BF16),
+            pltpu.VMEM((4, 4, 8, 512), BF16),
+            pltpu.VMEM((4, 4, 8, 512), BF16),
+            pltpu.VMEM((4, 4, 8, 512), BF16),
         ]
         + landing_shapes()
         + [
-            dma((32,)), dma,
+            dma((32,)),
             dma((3, 10)), dma((3, 10)), dma((3, 4)), dma((3, 4)),
             dma((4,)), dma((4,)), dma((3, 12)), dma((3, 12)),
+            dma((10,)), dma((10,)),
         ],
         compiler_params=pltpu.CompilerParams(
             collective_id=0, has_side_effects=True, vmem_limit_bytes=67_000_000
         ),
         name="gather_grad_project",
-    )(new_owner, places, tokens, cotangent, shard)
+    )(
+        new_owner, inverse, new_owner.reshape(1, 32), old_owner.reshape(1, 128),
+        tokens, cotangent, old_weight, old_first, old_second,
+    )
 
 
 def body(tokens, cotangent, old_weight, old_first, old_second, old_owner, new_owner):
-    devices, shards, groups, strip = 128, 32, 4, 256
-    slot_ids = jnp.arange(devices, dtype=jnp.int32)
+    slot_ids = jnp.arange(128, dtype=jnp.int32)
+    at = (slot_ids % 32) * 4 + slot_ids // 32
     inverse = jnp.sum(
-        jnp.where(old_owner[None, :] == slot_ids[:, None], slot_ids[None, :], 0), axis=1
+        jnp.where(old_owner[None, :] == slot_ids[:, None], at[None, :], 0), axis=1
     ).astype(jnp.int32)
-    r, f = inverse // shards, inverse % shards
-    places = jnp.stack([f // 8, (f // 2) % 4, f % 2, r // 2, r % 2], axis=1)
-    placing = (new_owner[None, :] * groups + jnp.arange(groups, dtype=jnp.int32)[:, None]).reshape(devices)
-
-    shard = old_weight.reshape(devices, strip)
-    stacked = jnp.concatenate(
-        [old_first.reshape(devices, strip).astype(BF16), old_second.reshape(devices, strip).astype(BF16), shard],
-        axis=1,
+    projected, gradient, moments, weight_rows = fused(
+        new_owner, inverse, old_owner, tokens, cotangent, old_weight, old_first, old_second
     )
-    outgoing = jnp.take(stacked, placing, axis=0)
-    arrived = lax.all_to_all(outgoing, ("rep", "fsdp"), split_axis=0, concat_axis=0, tiled=True)
-    projected, gradient = fused(new_owner, places, tokens, cotangent, shard)
-    moved = jnp.take(arrived, inverse, axis=0).astype(F32)
-    first_rows = moved[:, :strip].reshape(64, KV)
-    second_rows = moved[:, strip : 2 * strip].reshape(64, KV)
-    weight_rows = moved[:, 2 * strip :].reshape(64, KV)
-
-    first_next = beta_one * first_rows + (1.0 - beta_one) * gradient
-    second_next = beta_two * second_rows + (1.0 - beta_two) * gradient * gradient
+    first_next = beta_one * moments[0].astype(F32) + (1.0 - beta_one) * gradient
+    second_next = beta_two * moments[1].astype(F32) + (1.0 - beta_two) * gradient * gradient
     step_size = first_next / correction_one / (jnp.sqrt(second_next / correction_two) + epsilon)
-    updated = (weight_rows * (1.0 - learn_rate * decay_rate) - learn_rate * step_size).astype(BF16)
+    updated = (weight_rows.astype(F32) * (1.0 - learn_rate * decay_rate) - learn_rate * step_size).astype(BF16)
     return (projected, updated, first_next, second_next)
 
 

time: 97.9 us -> 87.6 us (0.89); the launches traced: 96.1 us -> 87.4 us
  Pallas kernels: 68.7 us -> 81.5 us
  starting transfers between devices: 11.9 us -> 0 us
  local copies, waits for them, and re-layouts: 8.72 us -> 2.26 us
  other arithmetic: 5.97 us -> 3.03 us
    pallas_call x1, Pallas kernels: 68.7 us -> 81.5 us  [fused(): pl.pallas_call(kernel, out_shape=(jax.ShapeDtypeStruct((ROWS, KV), BF16),...]
    all_to_all x1 -> x0, starting transfers between devices: 11.9 us -> none  [body(): lax.all_to_all(outgoing, ('rep', 'fsdp'), split_axis=0, concat_axis=0, ti...]
    unnamed x6 -> x1, local copies, waits for them, and re-layouts: 4.58 us -> 2.26 us
    convert_element_type x4 -> x1, other arithmetic: 3.61 us -> 1.74 us  [body(): (weight_rows.astype(F32) * (1.0 - learn_rate * decay_rate) - learn_rate *...]
    gather x2 -> x0, local copies, waits for them, and re-layouts: 1.74 us -> none  [the longest x1 0.87 us: body(): outgoing = jnp.take(stacked, placing, axis=0)]
  transfers between devices with their start and end apart: 1 -> 0, of which waited for: 0 -> 0; matrix products, arithmetic and copies ran while one was open for 2% -> 0% of each run, Pallas kernels for 71% -> 0%
where the time goes in v2:
time: 87.6 us; the launch traced here: 87.4 us
  Pallas kernels  81.5 us (93%)
  other arithmetic  3.03 us (3%)
  local copies, waits for them, and re-layouts  2.26 us (3%)
    pallas_call x1, Pallas kernels, fused(): pl.pallas_call(kernel, out_shape=(jax.ShapeDtypeStruct((ROWS, KV), BF16),...  81.5 us
    unnamed x1, local copies, waits for them, and re-layouts  2.26 us

profile of v2, /device:TPU:1, one launch (start us, length us, event | category | flops | bytes accessed | tf_op | source)
XLA Modules:
  0.0 87.4 jit_solution(13123203764511894601)
XLA Ops:
  0.6 1.3 %select_reduce_fusion.inv_ref = s32[128]{0:T(128)} fusion(s32[128]{0:T(128)S(1)} %fusion.2, s32[128]{0:T(128)} %param.12), kind=kLoop, calls=%fused_computation.4 | loop fusion | flops 49024 | bytes 1536 | tf_op jit(solution)/shard_map/reduce_sum | solution.py:568
  1.9 81.5 %gather_grad_project.1 = (bf16[1024,512]{1,0:T(8,128)(2,1)}, f32[64,512]{1,0:T(8,128)}, bf16[2,64,512]{2,1,0:T(8,128)(2,1)}, bf16[64,512]{1,0:T(8,128)(2,1)}) custom-call(s32[32]{0:T(128)} %nown_ref.1, s32[128]{0:T(128)} %select_reduce_fusion.inv_ref, s32[1,32]{1,0:T(1,128)} %bitcast.8, s32[1,128]{1,0:T(1,128)} %bitcast.9, bf16[1024,8192]{1,0:T(8,128)(2,1)} %tok_hbm.1, ...), custom_call_target="tpu_custom_call" | custom-call | tf_op jit(solution)/shard_map/gather_grad_project/pallas_call | solution.py:524
  83.4 1.7 %subtract_convert_fusion = (bf16[64,512]{1,0:T(8,128)(2,1)}, f32[64,512]{1,0:T(8,128)}, f32[64,512]{1,0:T(8,128)}) fusion(bf16[64,512]{1,0:T(8,128)(2,1)} %get-tuple-element.9, f32[64,512]{1,0:T(8,128)} %get-tuple-element.11, bf16[2,64,512]{2,1,0:T(8,128)(2,1)} %get-tuple-element.10), kind=kLoop, calls=%fused_computation.3 | loop fusion | flops 589824 | bytes 655360 | tf_op jit(solution)/shard_map/convert_element_type | solution.py:577
  85.1 2.3 %copy.12 = bf16[1024,512]{1,0:T(8,128)(2,1)} copy(bf16[1024,512]{1,0:T(8,128)(2,1)} %get-tuple-element.19) | data formatting | bytes 2097152
  (1 shorter events, 0.0 us)

commit v3 on v2

--- a/solution.py
+++ b/solution.py
@@ -93,11 +93,11 @@
 
     def step(n, carry):
         i3 = lax.rem(n, sizes[3])
-        n = n // sizes[3]
+        n = lax.div(n, sizes[3])
         i2 = lax.rem(n, sizes[2])
-        n = n // sizes[2]
+        n = lax.div(n, sizes[2])
         i1 = lax.rem(n, sizes[1])
-        i0 = n // sizes[1]
+        i0 = lax.div(n, sizes[1])
         i = (i0, i1, i2, i3)
         total = sources[0].ref[sources[0].index(i)].astype(F32)
         for s in sources[1:]:
@@ -178,6 +178,66 @@
     split = one_hot(iota(sq, 1) == lax.rem(iota(sq, 0), 2) * 64 + iota(sq, 0) // 2)
     G[x, z, yl, yh, core] = jnp.dot(split, stack_halves(w_ref[...]), preferred_element_type=F32).astype(BF16)
 
+    def gbox(spec, blocks):
+        starts, sizes = cut(spec)
+        lead = tuple(pl.ds(s, n) for s, n in zip(starts, sizes))
+        return G.at[lead + (pl.ds(core, 1), pl.ds(*blocks), slice(None))]
+
+    def ag_line(k):
+        axes, blocks = AG_COLORS[k]
+        a = axes[0]
+        box = gbox({t: ("at", me[t]) for t in axes}, blocks)
+        return [
+            send(box, box, ag_s.at[k, d - 1], ag_r.at[k, d - 1], device(**{a: ring(a, d)}))
+            for d in (1, 2, 3)
+        ]
+
+    def ag_plane(k):
+        axes, blocks = AG_COLORS[k]
+        a = axes[1]
+        box = gbox({axes[0]: ALL, a: ("at", me[a]), axes[2]: ("at", me[axes[2]])}, blocks)
+        return [
+            send(box, box, ag_s.at[k, 2 + d], ag_r.at[k, 2 + d], device(**{a: ring(a, d)}))
+            for d in (1, 2, 3)
+        ]
+
+    def ag_box(k, at, half=None):
+        axes, blocks = AG_COLORS[k]
+        first = ALL if half is None else ("half", half)
+        return gbox({axes[0]: first, axes[1]: ALL, axes[2]: ("at", at)}, blocks)
+
+    def ag_far(k):
+        a = AG_COLORS[k][0][2]
+        box = ag_box(k, me[a])
+        return [
+            send(box, box, ag_s.at[k, 6 + i], ag_r.at[k, 6 + i], device(**{a: ring(a, d)}))
+            for i, d in enumerate((1, 3))
+        ]
+
+    def ag_relay(k):
+        a = AG_COLORS[k][0][2]
+        up = ag_box(k, ring(a, 3), 0)
+        down = ag_box(k, ring(a, 1), 1)
+        return [
+            send(up, up, ag_s.at[k, 8], ag_r.at[k, 8], device(**{a: ring(a, 1)})),
+            send(down, down, ag_s.at[k, 9], ag_r.at[k, 9], device(**{a: ring(a, 3)})),
+        ]
+
+    def die(k, d):
+        a = AG_COLORS[k][0][2]
+        box = ag_box(k, ring(a, d))
+        return send(box, box, die_s.at[k, d], die_r.at[k, d], partner)
+
+    colors = range(3)
+    line = keep([c for k in colors for c in ag_line(k)])
+    plane = keep([c for k in colors for c in ag_plane(k)])
+    far = keep([c for k in colors for c in ag_far(k)])
+    relay = keep([c for k in colors for c in ag_relay(k)])
+    dies = [keep([die(k, d) for k in colors]) for d in range(4)]
+
+    pl.semaphore_wait(barrier, 10)
+    start(line)
+
     d = iota(sq, 1)
     dc, dyl, dyh, dx, dz = d // 64, lax.rem(d // 32, 2), lax.rem(d // 16, 2), lax.rem(d // 4, 4), lax.rem(d, 4)
     pick = one_hot((iota(sq, 0) == dx * 8 + dz * 2 + dyl)[:32])
@@ -191,66 +251,6 @@
     moved = lax.dot_general(choose, moments, (((0,), (0,)), ((), ())), preferred_element_type=F32).astype(BF16)
     for i in range(8):
         M0[i // 4, (i // 2) % 2, i % 2] = moved[16 * i : 16 * i + 16]
-
-    def gbox(spec, blocks):
-        starts, sizes = cut(spec)
-        lead = tuple(pl.ds(s, n) for s, n in zip(starts, sizes))
-        return G.at[lead + (pl.ds(core, 1), pl.ds(*blocks), slice(None))]
-
-    def ag_line(k):
-        axes, blocks = AG_COLORS[k]
-        a = axes[0]
-        box = gbox({t: ("at", me[t]) for t in axes}, blocks)
-        return [
-            send(box, box, ag_s.at[k, d - 1], ag_r.at[k, d - 1], device(**{a: ring(a, d)}))
-            for d in (1, 2, 3)
-        ]
-
-    def ag_plane(k):
-        axes, blocks = AG_COLORS[k]
-        a = axes[1]
-        box = gbox({axes[0]: ALL, a: ("at", me[a]), axes[2]: ("at", me[axes[2]])}, blocks)
-        return [
-            send(box, box, ag_s.at[k, 2 + d], ag_r.at[k, 2 + d], device(**{a: ring(a, d)}))
-            for d in (1, 2, 3)
-        ]
-
-    def ag_box(k, at, half=None):
-        axes, blocks = AG_COLORS[k]
-        first = ALL if half is None else ("half", half)
-        return gbox({axes[0]: first, axes[1]: ALL, axes[2]: ("at", at)}, blocks)
-
-    def ag_far(k):
-        a = AG_COLORS[k][0][2]
-        box = ag_box(k, me[a])
-        return [
-            send(box, box, ag_s.at[k, 6 + i], ag_r.at[k, 6 + i], device(**{a: ring(a, d)}))
-            for i, d in enumerate((1, 3))
-        ]
-
-    def ag_relay(k):
-        a = AG_COLORS[k][0][2]
-        up = ag_box(k, ring(a, 3), 0)
-        down = ag_box(k, ring(a, 1), 1)
-        return [
-            send(up, up, ag_s.at[k, 8], ag_r.at[k, 8], device(**{a: ring(a, 1)})),
-            send(down, down, ag_s.at[k, 9], ag_r.at[k, 9], device(**{a: ring(a, 3)})),
-        ]
-
-    def die(k, d):
-        a = AG_COLORS[k][0][2]
-        box = ag_box(k, ring(a, d))
-        return send(box, box, die_s.at[k, d], die_r.at[k, d], partner)
-
-    colors = range(3)
-    line = keep([c for k in colors for c in ag_line(k)])
-    plane = keep([c for k in colors for c in ag_plane(k)])
-    far = keep([c for k in colors for c in ag_far(k)])
-    relay = keep([c for k in colors for c in ag_relay(k)])
-    dies = [keep([die(k, d) for k in colors]) for d in range(4)]
-
-    pl.semaphore_wait(barrier, 10)
-    start(line)
 
     mv_c = keep([send(M0.at[1 - core], C1.at[core], mv_s.at[0], mv_r.at[0], partner)])
     start(mv_c)
@@ -273,20 +273,17 @@
 
     arrived(line)
     start(plane)
-    arrived(mv_c)
-    start(mv_y)
-    Y1[yl, yh] = C1[:, yl, yh]
     for c in tok_copies:
         c.wait()
 
     def grad_step(n, carry):
-        g = n // 8
+        g = lax.div(n, 8)
         m = lax.rem(n, 8)
         block = lax.dot_general(
             tok[nown_ref[n]], cot_ref[...], (((0,), (0,)), ((), ())), preferred_element_type=F32
         ).astype(BF16)
         for i in range(4):
-            part[g, m // 2, lax.rem(m, 2), i // 2, i % 2] = block[64 * i : 64 * i + 64]
+            part[g, lax.div(m, 2), lax.rem(m, 2), i // 2, i % 2] = block[64 * i : 64 * i + 64]
         return carry
 
     exchange = keep([
@@ -295,40 +292,36 @@
     ])
 
     def gradient(lo, hi):
-        lax.fori_loop(lo, hi, grad_step, 0, unroll=4)
+        lax.fori_loop(lo, hi, grad_step, 0, unroll=8)
 
     gradient(0, 8)
     exchange[0].start()
+    arrived(mv_c)
+    start(mv_y)
+    Y1[yl, yh] = C1[:, yl, yh]
+    gradient(8, 16)
+    exchange[1].start()
     arrived(plane)
     start(far)
     start(dies[0])
+    gradient(16, 24)
+    exchange[2].start()
     arrived(mv_y)
     rows = Y1[...].reshape(128, 512)
     swap = one_hot(iota(sq, 1) == lax.rem(iota(sq, 0), 8) * 16 + iota(sq, 0) // 8)
     XZ[...] = jnp.dot(swap, rows, preferred_element_type=F32).astype(BF16).reshape(4, 4, 8, 512)
     start(mv_x)
     X1[x] = XZ[x]
-    gradient(8, 16)
-    exchange[1].start()
-    gradient(16, 24)
-    exchange[2].start()
-    arrived(mv_x)
-    start(mv_z)
-    Z1[:, z] = X1[:, z]
     gradient(24, 32)
     exchange[3].start()
-    arrived(far)
-    start(relay)
-    start(dies[1])
-    start(dies[3])
 
     def chip_sum(g):
         exchange[g].wait_recv()
 
         def step(n, carry):
             i3 = lax.rem(n, 2)
-            i2 = lax.rem(n // 2, 2)
-            i1 = n // 4
+            i2 = lax.rem(lax.div(n, 2), 2)
+            i1 = lax.div(n, 4)
             S[g, i1, i2, i3] = (
                 part[g, i1, i2, i3, core].astype(F32) + recv[g, i1, i2, i3].astype(F32)
             ).astype(BF16)
@@ -415,24 +408,31 @@
     fourth = keep([c for p in plans for c in p[6]])
 
     start(first)
+    arrived(far)
+    start(relay)
+    start(dies[1])
+    start(dies[3])
+    arrived(mv_x)
+    start(mv_z)
+    Z1[:, z] = X1[:, z]
 
     arrived(relay)
     start(dies[2])
 
-    def place(s, b):
+    def slot(s):
         i = inv_ref[s]
-        return G[
-            i // 32, lax.rem(i // 8, 4), lax.rem(i // 4, 2), lax.rem(i // 2, 2), lax.rem(i, 2),
-            pl.ds(pl.multiple_of(b, 16), 16), :,
-        ]
+        return (
+            lax.div(i, 32), lax.rem(lax.div(i, 8), 4), lax.rem(lax.div(i, 4), 2), lax.rem(lax.div(i, 2), 2), lax.rem(i, 2),
+        )
 
     def assemble(n, carry):
-        b0 = (n // 4) * 16
-        j0 = lax.rem(n, 4) * 16
+        j0 = pl.multiple_of(n * 16, 16)
         for h in range(2):
-            got = jnp.swapaxes(jnp.stack([place(2 * (j0 + t) + h, b0) for t in range(16)], axis=0), 0, 1)
-            for b in range(16):
-                W[b0 + b, pl.ds(pl.multiple_of(j0, 16), 16), pl.ds(256 * h, 256)] = got[b]
+            slots = [slot(2 * (n * 16 + t) + h) for t in range(16)]
+            for b0 in range(0, 128, 16):
+                got = jnp.swapaxes(jnp.stack([G[i + (pl.ds(b0, 16), slice(None))] for i in slots], axis=0), 0, 1)
+                for b in range(16):
+                    W[b0 + b, pl.ds(j0, 16), pl.ds(256 * h, 256)] = got[b]
         return carry
 
     def project(m):
@@ -444,7 +444,7 @@
 
     for d in (0, 1, 3, 2):
         arrived(dies[d])
-    lax.fori_loop(0, 32, assemble, 0)
+    lax.fori_loop(0, 4, assemble, 0)
     for p in plans:
         arrived(p[0][:2])
         p[1]()

time: 87.6 us -> 74.7 us (0.85)
  Pallas kernels: 81.5 us -> 68.1 us
    pallas_call x1, Pallas kernels: 81.5 us -> 68.1 us  [fused(): pl.pallas_call(kernel, out_shape=(jax.ShapeDtypeStruct((ROWS, KV), BF16),...]
where the time goes in v3:
time: 74.7 us; the launch traced here: 74 us
  Pallas kernels  68.1 us (91%)
  other arithmetic  3.03 us (4%)
  local copies, waits for them, and re-layouts  2.26 us (3%)
    pallas_call x1, Pallas kernels, fused(): pl.pallas_call(kernel, out_shape=(jax.ShapeDtypeStruct((ROWS, KV), BF16),...  68.1 us
    unnamed x1, local copies, waits for them, and re-layouts  2.26 us
    convert_element_type x1, other arithmetic, body(): (weight_rows.astype(F32) * (1.0 - learn_rate * decay_rate) - learn_rate *...  1.74 us

profile of v3, /device:TPU:1, one launch (start us, length us, event | category | flops | bytes accessed | tf_op | source)
XLA Modules:
  0.0 74.0 jit_solution(13825262200108756518)
XLA Ops:
  0.6 1.3 %select_reduce_fusion.inv_ref = s32[128]{0:T(128)} fusion(s32[128]{0:T(128)S(1)} %fusion.2, s32[128]{0:T(128)} %param.12), kind=kLoop, calls=%fused_computation.4 | loop fusion | flops 49024 | bytes 1536 | tf_op jit(solution)/shard_map/reduce_sum | solution.py:568
  1.9 68.1 %gather_grad_project.1 = (bf16[1024,512]{1,0:T(8,128)(2,1)}, f32[64,512]{1,0:T(8,128)}, bf16[2,64,512]{2,1,0:T(8,128)(2,1)}, bf16[64,512]{1,0:T(8,128)(2,1)}) custom-call(s32[32]{0:T(128)} %nown_ref.1, s32[128]{0:T(128)} %select_reduce_fusion.inv_ref, s32[1,32]{1,0:T(1,128)} %bitcast.8, s32[1,128]{1,0:T(1,128)} %bitcast.9, bf16[1024,8192]{1,0:T(8,128)(2,1)} %tok_hbm.1, ...), custom_call_target="tpu_custom_call" | custom-call | tf_op jit(solution)/shard_map/gather_grad_project/pallas_call | solution.py:524
  70.0 1.7 %subtract_convert_fusion = (bf16[64,512]{1,0:T(8,128)(2,1)}, f32[64,512]{1,0:T(8,128)}, f32[64,512]{1,0:T(8,128)}) fusion(bf16[64,512]{1,0:T(8,128)(2,1)} %get-tuple-element.9, f32[64,512]{1,0:T(8,128)} %get-tuple-element.11, bf16[2,64,512]{2,1,0:T(8,128)(2,1)} %get-tuple-element.10), kind=kLoop, calls=%fused_computation.3 | loop fusion | flops 589824 | bytes 655360 | tf_op jit(solution)/shard_map/convert_element_type | solution.py:577
  71.8 2.3 %copy.12 = bf16[1024,512]{1,0:T(8,128)(2,1)} copy(bf16[1024,512]{1,0:T(8,128)(2,1)} %get-tuple-element.19) | data formatting | bytes 2097152
  (1 shorter events, 0.0 us)

commit v4 on v3

--- a/solution.py
+++ b/solution.py
@@ -121,8 +121,9 @@
 
 
 def kernel(
-    nown_ref, inv_ref, nown_vec, owner_vec, tok_hbm, cot_ref, w_ref, first_ref, second_ref,
-    out_ref, grad_ref, m_ref, wrow_ref,
+    nown_ref, inv_ref, nown_vec, owner_vec, tok_hbm, cot_hbm, first_hbm, second_hbm, w_ref,
+    out_hbm, grad_ref, m_ref, wrow_ref,
+    cot_ref, first_ref, second_ref, out_v, in_sem, out_sem,
     tok, G, W, part, recv, S,
     M0, C1, Y1, XZ, X1, Z1,
     *rest,
@@ -172,6 +173,11 @@
         pltpu.make_async_copy(tok_hbm.at[:, pl.ds(256 * q, 256)], tok.at[q], tok_sem.at[q])
         for q in range(32)
     ]
+    in_copies = [
+        pltpu.make_async_copy(a, b, in_sem.at[i])
+        for i, (a, b) in enumerate(((first_hbm, first_ref), (second_hbm, second_ref), (cot_hbm, cot_ref)))
+    ]
+    start(in_copies)
     start(tok_copies)
 
     sq = (128, 128)
@@ -245,6 +251,8 @@
     block = block + (dyh * 2 + dc)[:1].astype(F32)
     sp = iota(sq, 0)
     choose = one_hot(block == (2 * lax.rem(sp, 64) + sp // 64).astype(F32))
+    in_copies[0].wait()
+    in_copies[1].wait()
     moments = jnp.concatenate(
         [stack_halves(first_ref[...].astype(BF16)), stack_halves(second_ref[...].astype(BF16))], axis=1
     )
@@ -273,6 +281,7 @@
 
     arrived(line)
     start(plane)
+    in_copies[2].wait()
     for c in tok_copies:
         c.wait()
 
@@ -402,19 +411,25 @@
         return first, fold_first, second, fold_second, third, fold_third, fourth, fold_fourth
 
     plans = [rs(k) for k in colors]
-    first = keep([c for p in plans for c in p[0]])
+    early = keep([c for p in plans for c in p[0][:2]])
+    raw = keep([c for p in plans for c in p[0][2:]])
     second = keep([c for p in plans for c in p[2]])
     third = keep([c for p in plans for c in p[4]])
     fourth = keep([c for p in plans for c in p[6]])
 
-    start(first)
+    start(early)
     arrived(far)
     start(relay)
     start(dies[1])
     start(dies[3])
+    start(raw)
     arrived(mv_x)
     start(mv_z)
     Z1[:, z] = X1[:, z]
+    for p in plans:
+        arrived(p[0][:2])
+        p[1]()
+        start(p[2])
 
     arrived(relay)
     start(dies[2])
@@ -435,32 +450,32 @@
                     W[b0 + b, pl.ds(j0, 16), pl.ds(256 * h, 256)] = got[b]
         return carry
 
+    leave = [
+        pltpu.make_async_copy(out_v.at[m % 2], out_hbm.at[pl.ds(256 * m, 256), :], out_sem.at[m]) for m in range(4)
+    ]
+
     def project(m):
-        at = 256 * m
-        rows = jnp.concatenate([tok[q, pl.ds(at, 256), :] for q in range(32)], axis=1)
-        out_ref[pl.ds(at, 256), :] = jnp.dot(
-            rows, W[...].reshape(D, KV), preferred_element_type=F32
-        ).astype(BF16)
+        rows = jnp.concatenate([tok[q, pl.ds(256 * m, 256), :] for q in range(32)], axis=1)
+        if m >= 2:
+            leave[m - 2].wait()
+        out_v[m % 2] = jnp.dot(rows, W[...].reshape(D, KV), preferred_element_type=F32)
+        leave[m].start()
 
     for d in (0, 1, 3, 2):
         arrived(dies[d])
     lax.fori_loop(0, 4, assemble, 0)
-    for p in plans:
-        arrived(p[0][:2])
-        p[1]()
-        start(p[2])
     project(0)
-    project(1)
     for p in plans:
         arrived(p[0][2:] + p[2])
         p[3]()
         start(p[4])
+    project(1)
     project(2)
-    project(3)
     for p in plans:
         arrived(p[4])
         p[5]()
         start(p[6])
+    project(3)
 
     arrived(mv_z)
     owner = jnp.dot(
@@ -482,6 +497,8 @@
     for p in plans:
         arrived(p[6])
         p[7]()
+    leave[2].wait()
+    leave[3].wait()
     for c in everything:
         c.wait_send()
 
@@ -520,18 +537,25 @@
 def fused(new_owner, inverse, old_owner, tokens, cotangent, old_weight, old_first, old_second):
     smem = pl.BlockSpec(memory_space=pltpu.SMEM)
     vmem = pl.BlockSpec(memory_space=pltpu.VMEM)
+    anywhere = pl.BlockSpec(memory_space=pl.ANY)
     dma = pltpu.SemaphoreType.DMA
     return pl.pallas_call(
         kernel,
         out_shape=(
-            jax.ShapeDtypeStruct((ROWS, KV), BF16),
+            jax.ShapeDtypeStruct((ROWS, KV), F32),
             jax.ShapeDtypeStruct((64, KV), F32),
             jax.ShapeDtypeStruct((2, 64, KV), BF16),
             jax.ShapeDtypeStruct((64, KV), BF16),
         ),
-        in_specs=[smem, smem, vmem, vmem, pl.BlockSpec(memory_space=pl.ANY)] + [vmem] * 4,
-        out_specs=(vmem,) * 4,
+        in_specs=[smem, smem, vmem, vmem] + [anywhere] * 4 + [vmem],
+        out_specs=(anywhere, vmem, vmem, vmem),
         scratch_shapes=[
+            pltpu.VMEM((ROWS, KV), BF16),
+            pltpu.VMEM((64, KV), F32),
+            pltpu.VMEM((64, KV), F32),
+            pltpu.VMEM((2, 256, KV), F32),
+            dma((3,)),
+            dma((4,)),
             pltpu.VMEM((32, ROWS, 256), BF16),
             pltpu.VMEM((4, 4, 2, 2, 2, 128, 256), BF16),
             pltpu.VMEM((128, 64, KV), BF16),
@@ -558,7 +582,7 @@
         name="gather_grad_project",
     )(
         new_owner, inverse, new_owner.reshape(1, 32), old_owner.reshape(1, 128),
-        tokens, cotangent, old_weight, old_first, old_second,
+        tokens, cotangent, old_first, old_second, old_weight,
     )
 
 
@@ -575,7 +599,7 @@
     second_next = beta_two * moments[1].astype(F32) + (1.0 - beta_two) * gradient * gradient
     step_size = first_next / correction_one / (jnp.sqrt(second_next / correction_two) + epsilon)
     updated = (weight_rows.astype(F32) * (1.0 - learn_rate * decay_rate) - learn_rate * step_size).astype(BF16)
-    return (projected, updated, first_next, second_next)
+    return (projected.astype(BF16), updated, first_next, second_next)
 
 
 def solution(mesh):

time: 74.7 us -> 68.1 us (0.912)
  Pallas kernels: 68.1 us -> 61.6 us
  other arithmetic: 3.03 us -> 5.72 us
  local copies, waits for them, and re-layouts: 2.26 us -> 0 us
    pallas_call x1, Pallas kernels: 68.1 us -> 61.6 us  [fused(): pl.pallas_call(kernel, out_shape=(jax.ShapeDtypeStruct((ROWS, KV), F32),...]
    convert_element_type x0 -> x1, other arithmetic: none -> 2.69 us  [body(): return (projected.astype(BF16), updated, first_next, second_next)]
    unnamed x1 -> x0, local copies, waits for them, and re-layouts: 2.26 us -> none
where the time goes in v4:
time: 68.1 us; the launch traced here: 67.9 us
  Pallas kernels  61.6 us (90%)
  other arithmetic  5.72 us (8%)
    pallas_call x1, Pallas kernels, fused(): pl.pallas_call(kernel, out_shape=(jax.ShapeDtypeStruct((ROWS, KV), F32),...  61.6 us
    convert_element_type x1, other arithmetic, body(): return (projected.astype(BF16), updated, first_next, second_next)  2.69 us
    convert_element_type x1, other arithmetic, body(): (weight_rows.astype(F32) * (1.0 - learn_rate * decay_rate) - learn_rate *...  1.74 us

profile of v4, /device:TPU:1, one launch (start us, length us, event | category | flops | bytes accessed | tf_op | source)
XLA Modules:
  0.0 67.9 jit_solution(13873488882853214995)
XLA Ops:
  0.6 1.3 %select_reduce_fusion.inv_ref = s32[128]{0:T(128)} fusion(s32[128]{0:T(128)S(1)} %fusion.2, s32[128]{0:T(128)} %param.12), kind=kLoop, calls=%fused_computation.4 | loop fusion | flops 49024 | bytes 1536 | tf_op jit(solution)/shard_map/reduce_sum | solution.py:592
  1.9 61.6 %gather_grad_project.1 = (f32[1024,512]{1,0:T(8,128)}, f32[64,512]{1,0:T(8,128)}, bf16[2,64,512]{2,1,0:T(8,128)(2,1)}, bf16[64,512]{1,0:T(8,128)(2,1)}) custom-call(s32[32]{0:T(128)} %nown_ref.1, s32[128]{0:T(128)} %select_reduce_fusion.inv_ref, s32[1,32]{1,0:T(1,128)} %bitcast.8, s32[1,128]{1,0:T(1,128)} %bitcast.9, bf16[1024,8192]{1,0:T(8,128)(2,1)} %tok_hbm.1, ...), custom_call_target="tpu_custom_call" | custom-call | tf_op jit(solution)/shard_map/gather_grad_project/pallas_call | solution.py:542
  63.5 2.7 %convert_element_type.17 = bf16[1024,512]{1,0:T(8,128)(2,1)} convert(f32[1024,512]{1,0:T(8,128)} %get-tuple-element.8) | non-fusion elementwise | flops 524288 | bytes 3145728 | tf_op jit(solution)/shard_map/convert_element_type | solution.py:602
  66.2 1.7 %subtract_convert_fusion = (bf16[64,512]{1,0:T(8,128)(2,1)}, f32[64,512]{1,0:T(8,128)}, f32[64,512]{1,0:T(8,128)}) fusion(bf16[64,512]{1,0:T(8,128)(2,1)} %get-tuple-element.9, f32[64,512]{1,0:T(8,128)} %get-tuple-element.11, bf16[2,64,512]{2,1,0:T(8,128)(2,1)} %get-tuple-element.10), kind=kLoop, calls=%fused_computation.3 | loop fusion | flops 589824 | bytes 655360 | tf_op jit(solution)/shard_map/convert_element_type | solution.py:601
  (1 shorter events, 0.0 us)

commit v5 on v4

--- a/solution.py
+++ b/solution.py
@@ -121,9 +121,9 @@
 
 
 def kernel(
-    nown_ref, inv_ref, nown_vec, owner_vec, tok_hbm, cot_hbm, first_hbm, second_hbm, w_ref,
+    nown_ref, nown_vec, owner_vec, tok_hbm, cot_hbm, first_hbm, second_hbm, w_ref,
     out_hbm, grad_ref, m_ref, wrow_ref,
-    cot_ref, first_ref, second_ref, out_v, in_sem, out_sem,
+    cot_ref, first_ref, second_ref, out_v, in_sem, out_sem, inv_vec, inv_ref, inv_sem,
     tok, G, W, part, recv, S,
     M0, C1, Y1, XZ, X1, Z1,
     *rest,
@@ -243,6 +243,11 @@
 
     pl.semaphore_wait(barrier, 10)
     start(line)
+
+    at = lax.rem(iota(sq, 1), 32) * 4 + iota(sq, 1) // 32
+    column = jnp.max(jnp.where(owner_vec[...] == iota(sq, 0), at, 0), axis=1, keepdims=True)
+    inv_vec[...] = jnp.max(jnp.where(iota(sq, 0) == iota(sq, 1), column, 0), axis=0, keepdims=True)
+    inv_copy = pltpu.make_async_copy(inv_vec, inv_ref, inv_sem)
 
     d = iota(sq, 1)
     dc, dyl, dyh, dx, dz = d // 64, lax.rem(d // 32, 2), lax.rem(d // 16, 2), lax.rem(d // 4, 4), lax.rem(d, 4)
@@ -263,6 +268,7 @@
     mv_c = keep([send(M0.at[1 - core], C1.at[core], mv_s.at[0], mv_r.at[0], partner)])
     start(mv_c)
     C1[core] = M0[core]
+    inv_copy.start()
     mv_y = keep([
         send(
             C1.at[:, lax.rem(ring("y", d), 2), ring("y", d) // 2], Y1.at[yl, yh],
@@ -435,7 +441,7 @@
     start(dies[2])
 
     def slot(s):
-        i = inv_ref[s]
+        i = inv_ref[0, s]
         return (
             lax.div(i, 32), lax.rem(lax.div(i, 8), 4), lax.rem(lax.div(i, 4), 2), lax.rem(lax.div(i, 2), 2), lax.rem(i, 2),
         )
@@ -458,11 +464,12 @@
         rows = jnp.concatenate([tok[q, pl.ds(256 * m, 256), :] for q in range(32)], axis=1)
         if m >= 2:
             leave[m - 2].wait()
-        out_v[m % 2] = jnp.dot(rows, W[...].reshape(D, KV), preferred_element_type=F32)
+        out_v[m % 2] = jnp.dot(rows, W[...].reshape(D, KV), preferred_element_type=F32).astype(BF16)
         leave[m].start()
 
     for d in (0, 1, 3, 2):
         arrived(dies[d])
+    inv_copy.wait()
     lax.fori_loop(0, 4, assemble, 0)
     project(0)
     for p in plans:
@@ -534,7 +541,7 @@
     return sizes
 
 
-def fused(new_owner, inverse, old_owner, tokens, cotangent, old_weight, old_first, old_second):
+def fused(new_owner, old_owner, tokens, cotangent, old_weight, old_first, old_second):
     smem = pl.BlockSpec(memory_space=pltpu.SMEM)
     vmem = pl.BlockSpec(memory_space=pltpu.VMEM)
     anywhere = pl.BlockSpec(memory_space=pl.ANY)
@@ -542,20 +549,23 @@
     return pl.pallas_call(
         kernel,
         out_shape=(
-            jax.ShapeDtypeStruct((ROWS, KV), F32),
+            jax.ShapeDtypeStruct((ROWS, KV), BF16),
             jax.ShapeDtypeStruct((64, KV), F32),
             jax.ShapeDtypeStruct((2, 64, KV), BF16),
             jax.ShapeDtypeStruct((64, KV), BF16),
         ),
-        in_specs=[smem, smem, vmem, vmem] + [anywhere] * 4 + [vmem],
+        in_specs=[smem, vmem, vmem] + [anywhere] * 4 + [vmem],
         out_specs=(anywhere, vmem, vmem, vmem),
         scratch_shapes=[
             pltpu.VMEM((ROWS, KV), BF16),
             pltpu.VMEM((64, KV), F32),
             pltpu.VMEM((64, KV), F32),
-            pltpu.VMEM((2, 256, KV), F32),
+            pltpu.VMEM((2, 256, KV), BF16),
             dma((3,)),
             dma((4,)),
+            pltpu.VMEM((1, 128), jnp.int32),
+            pltpu.SMEM((1, 128), jnp.int32),
+            dma,
             pltpu.VMEM((32, ROWS, 256), BF16),
             pltpu.VMEM((4, 4, 2, 2, 2, 128, 256), BF16),
             pltpu.VMEM((128, 64, KV), BF16),
@@ -581,25 +591,72 @@
         ),
         name="gather_grad_project",
     )(
-        new_owner, inverse, new_owner.reshape(1, 32), old_owner.reshape(1, 128),
+        new_owner, new_owner.reshape(1, 32), old_owner.reshape(1, 128),
         tokens, cotangent, old_first, old_second, old_weight,
     )
 
 
+def finish_kernel(
+    proj_hbm, grad_hbm, m_hbm, w_hbm, out_hbm, new_w_hbm, new_f_hbm, new_s_hbm,
+    proj, grad, m, w, new_w, new_f, new_s, in_sem, out_sem,
+):
+    tiles = [pl.ds(256 * i, 256) for i in range(4)]
+    small = [
+        pltpu.make_async_copy(a, b, in_sem.at[i])
+        for i, (a, b) in enumerate(((grad_hbm, grad), (m_hbm, m), (w_hbm, w)))
+    ]
+    enter = [pltpu.make_async_copy(proj_hbm.at[t], proj.at[t], in_sem.at[3 + i]) for i, t in enumerate(tiles)]
+    leave = [pltpu.make_async_copy(proj.at[t], out_hbm.at[t], out_sem.at[3 + i]) for i, t in enumerate(tiles)]
+    results = [
+        pltpu.make_async_copy(a, b, out_sem.at[i])
+        for i, (a, b) in enumerate(((new_w, new_w_hbm), (new_f, new_f_hbm), (new_s, new_s_hbm)))
+    ]
+    for c in small + enter:
+        c.start()
+    for c in small:
+        c.wait()
+    gradient = grad[...]
+    first_next = beta_one * m[0].astype(F32) + (1.0 - beta_one) * gradient
+    second_next = beta_two * m[1].astype(F32) + (1.0 - beta_two) * gradient * gradient
+    step_size = first_next / correction_one / (jnp.sqrt(second_next / correction_two) + epsilon)
+    new_f[...] = first_next
+    new_s[...] = second_next
+    new_w[...] = (w[...].astype(F32) * (1.0 - learn_rate * decay_rate) - learn_rate * step_size).astype(BF16)
+    for a, b in zip(enter, leave):
+        a.wait()
+        b.start()
+    for c in results:
+        c.start()
+    for c in results + leave:
+        c.wait()
+
+
+def finish(projected, gradient, moments, weight_rows):
+    anywhere = pl.BlockSpec(memory_space=pl.ANY)
+    f32, bf16 = pltpu.VMEM((64, KV), F32), pltpu.VMEM((64, KV), BF16)
+    return pl.pallas_call(
+        finish_kernel,
+        out_shape=(
+            jax.ShapeDtypeStruct((ROWS, KV), BF16),
+            jax.ShapeDtypeStruct((64, KV), BF16),
+            jax.ShapeDtypeStruct((64, KV), F32),
+            jax.ShapeDtypeStruct((64, KV), F32),
+        ),
+        in_specs=[anywhere] * 4,
+        out_specs=(anywhere,) * 4,
+        scratch_shapes=[
+            pltpu.VMEM((ROWS, KV), BF16), f32, pltpu.VMEM((2, 64, KV), BF16), bf16, bf16, f32, f32,
+            pltpu.SemaphoreType.DMA((7,)), pltpu.SemaphoreType.DMA((7,)),
+        ],
+        name="adamw",
+    )(projected, gradient, moments, weight_rows)
+
+
 def body(tokens, cotangent, old_weight, old_first, old_second, old_owner, new_owner):
-    slot_ids = jnp.arange(128, dtype=jnp.int32)
-    at = (slot_ids % 32) * 4 + slot_ids // 32
-    inverse = jnp.sum(
-        jnp.where(old_owner[None, :] == slot_ids[:, None], at[None, :], 0), axis=1
-    ).astype(jnp.int32)
     projected, gradient, moments, weight_rows = fused(
-        new_owner, inverse, old_owner, tokens, cotangent, old_weight, old_first, old_second
+        new_owner, old_owner, tokens, cotangent, old_weight, old_first, old_second
     )
-    first_next = beta_one * moments[0].astype(F32) + (1.0 - beta_one) * gradient
-    second_next = beta_two * moments[1].astype(F32) + (1.0 - beta_two) * gradient * gradient
-    step_size = first_next / correction_one / (jnp.sqrt(second_next / correction_two) + epsilon)
-    updated = (weight_rows.astype(F32) * (1.0 - learn_rate * decay_rate) - learn_rate * step_size).astype(BF16)
-    return (projected.astype(BF16), updated, first_next, second_next)
+    return finish(projected, gradient, moments, weight_rows)
 
 
 def solution(mesh):

time: 68.1 us -> 64.8 us (0.952)
  other arithmetic: 5.72 us -> 0 us
  Pallas kernels: 61.6 us -> 63.8 us
    convert_element_type x2 -> x0, other arithmetic: 4.43 us -> none  [the longest x1 2.69 us: body(): return (projected.astype(BF16), updated, first_next, second_next)]
    pallas_call x1 -> x2, Pallas kernels: 61.6 us -> 63.8 us  [the longest x1 61.5 us: fused(): pl.pallas_call(kernel, out_shape=(jax.ShapeDtypeStruct((ROWS, KV), BF16),...]
    reduce_sum x1 -> x0, other arithmetic: 1.28 us -> none  [body(): jnp.sum(jnp.where(old_owner[None, :] == slot_ids[:, None], at[None, :], 0...]
where the time goes in v5:
time: 64.8 us; the launch traced here: 64.6 us
  Pallas kernels  63.8 us (98%)
  between operations  0.8 us (1%)
    pallas_call x1, Pallas kernels, fused(): pl.pallas_call(kernel, out_shape=(jax.ShapeDtypeStruct((ROWS, KV), BF16),...  61.5 us
    pallas_call x1, Pallas kernels, finish(): pl.pallas_call(finish_kernel, out_shape=(jax.ShapeDtypeStruct((ROWS, KV),...  2.31 us

profile of v5, /device:TPU:1, one launch (start us, length us, event | category | flops | bytes accessed | tf_op | source)
XLA Modules:
  0.0 64.6 jit_solution(12044597722561564323)
XLA Ops:
  0.6 61.5 %gather_grad_project.1 = (bf16[1024,512]{1,0:T(8,128)(2,1)}, f32[64,512]{1,0:T(8,128)}, bf16[2,64,512]{2,1,0:T(8,128)(2,1)}, bf16[64,512]{1,0:T(8,128)(2,1)}) custom-call(s32[32]{0:T(128)} %nown_ref.1, s32[1,32]{1,0:T(1,128)} %bitcast.2, s32[1,128]{1,0:T(1,128)} %bitcast.3, bf16[1024,8192]{1,0:T(8,128)(2,1)} %tok_hbm.1, bf16[1024,512]{1,0:T(8,128)(2,1)} %cot_hbm.1, ...), custom_call_target="tpu_custom_call" | custom-call | tf_op jit(solution)/shard_map/gather_grad_project/pallas_call | solution.py:549
  62.2 2.3 %adamw.1 = (bf16[1024,512]{1,0:T(8,128)(2,1)}, bf16[64,512]{1,0:T(8,128)(2,1)}, f32[64,512]{1,0:T(8,128)}, f32[64,512]{1,0:T(8,128)}) custom-call(bf16[1024,512]{1,0:T(8,128)(2,1)} %get-tuple-element.8.proj_hbm, f32[64,512]{1,0:T(8,128)} %get-tuple-element.9.grad_hbm, bf16[2,64,512]{2,1,0:T(8,128)(2,1)} %get-tuple-element.10.m_hbm, ...), custom_call_target="tpu_custom_call" | custom-call | tf_op jit(solution)/shard_map/adamw/pallas_call | solution.py:637

commit v6 on v5

--- a/solution.py
+++ b/solution.py
@@ -124,7 +124,7 @@
     nown_ref, nown_vec, owner_vec, tok_hbm, cot_hbm, first_hbm, second_hbm, w_ref,
     out_hbm, grad_ref, m_ref, wrow_ref,
     cot_ref, first_ref, second_ref, out_v, in_sem, out_sem, inv_vec, inv_ref, inv_sem,
-    tok, G, W, part, recv, S,
+    tok_a, tok_b, acc, G, W, part, recv, S,
     M0, C1, Y1, XZ, X1, Z1,
     *rest,
 ):
@@ -170,7 +170,10 @@
     pl.semaphore_signal(barrier, inc=1, device_id=partner, device_id_type=MESH)
 
     tok_copies = [
-        pltpu.make_async_copy(tok_hbm.at[:, pl.ds(256 * q, 256)], tok.at[q], tok_sem.at[q])
+        pltpu.make_async_copy(
+            tok_hbm.at[pl.ds(512 * h, 512), pl.ds(256 * q, 256)], tok.at[q], tok_sem.at[32 * h + q]
+        )
+        for h, tok in enumerate((tok_a, tok_b))
         for q in range(32)
     ]
     in_copies = [
@@ -288,18 +291,31 @@
     arrived(line)
     start(plane)
     in_copies[2].wait()
-    for c in tok_copies:
+    for c in tok_copies[:32]:
         c.wait()
+
+    def leave_block(n, g, m, block, carry):
+        block = block.astype(BF16)
+        for i in range(4):
+            part[g, lax.div(m, 2), lax.rem(m, 2), i // 2, i % 2] = block[64 * i : 64 * i + 64]
+        return carry
+
+    def contract(a, b):
+        return lax.dot_general(a, b, (((0,), (0,)), ((), ())), preferred_element_type=F32)
+
+    def grad_begin(n, carry):
+        acc[n] = contract(tok_a[nown_ref[n]], cot_ref[:512])
+        return carry
+
+    def grad_end(n, carry):
+        block = acc[n] + contract(tok_b[nown_ref[n]], cot_ref[512:])
+        return leave_block(n, 0, n, block, carry)
 
     def grad_step(n, carry):
         g = lax.div(n, 8)
         m = lax.rem(n, 8)
-        block = lax.dot_general(
-            tok[nown_ref[n]], cot_ref[...], (((0,), (0,)), ((), ())), preferred_element_type=F32
-        ).astype(BF16)
-        for i in range(4):
-            part[g, lax.div(m, 2), lax.rem(m, 2), i // 2, i % 2] = block[64 * i : 64 * i + 64]
-        return carry
+        both = jnp.concatenate([tok_a[nown_ref[n]], tok_b[nown_ref[n]]], axis=0)
+        return leave_block(n, g, m, contract(both, cot_ref[...]), carry)
 
     exchange = keep([
         send(part.at[g, :, :, :, 1 - core], recv.at[g], ex_s.at[g], ex_r.at[g], partner)
@@ -309,7 +325,10 @@
     def gradient(lo, hi):
         lax.fori_loop(lo, hi, grad_step, 0, unroll=8)
 
-    gradient(0, 8)
+    lax.fori_loop(0, 8, grad_begin, 0, unroll=8)
+    for c in tok_copies[32:]:
+        c.wait()
+    lax.fori_loop(0, 8, grad_end, 0, unroll=8)
     exchange[0].start()
     arrived(mv_c)
     start(mv_y)
@@ -461,7 +480,8 @@
     ]
 
     def project(m):
-        rows = jnp.concatenate([tok[q, pl.ds(256 * m, 256), :] for q in range(32)], axis=1)
+        tok = (tok_a, tok_b)[m // 2]
+        rows = jnp.concatenate([tok[q, pl.ds(256 * (m % 2), 256), :] for q in range(32)], axis=1)
         if m >= 2:
             leave[m - 2].wait()
         out_v[m % 2] = jnp.dot(rows, W[...].reshape(D, KV), preferred_element_type=F32).astype(BF16)
@@ -566,7 +586,9 @@
             pltpu.VMEM((1, 128), jnp.int32),
             pltpu.SMEM((1, 128), jnp.int32),
             dma,
-            pltpu.VMEM((32, ROWS, 256), BF16),
+            pltpu.VMEM((32, ROWS // 2, 256), BF16),
+            pltpu.VMEM((32, ROWS // 2, 256), BF16),
+            pltpu.VMEM((8, 256, KV), F32),
             pltpu.VMEM((4, 4, 2, 2, 2, 128, 256), BF16),
             pltpu.VMEM((128, 64, KV), BF16),
             pltpu.VMEM((4, 4, 2, 2, 2, 64, KV), BF16),
@@ -581,7 +603,7 @@
         ]
         + landing_shapes()
         + [
-            dma((32,)),
+            dma((64,)),
             dma((3, 10)), dma((3, 10)), dma((3, 4)), dma((3, 4)),
             dma((4,)), dma((4,)), dma((3, 12)), dma((3, 12)),
             dma((10,)), dma((10,)),

time: 64.8 us -> 65.1 us (level)
  no operation moved by 1% of the time
where the time goes in v6:
time: 65.1 us; the launch traced here: 65 us
  Pallas kernels  64.2 us (99%)
  between operations  0.8 us (1%)
    pallas_call x1, Pallas kernels, fused(): pl.pallas_call(kernel, out_shape=(jax.ShapeDtypeStruct((ROWS, KV), BF16),...  61.9 us
    pallas_call x1, Pallas kernels, finish(): pl.pallas_call(finish_kernel, out_shape=(jax.ShapeDtypeStruct((ROWS, KV),...  2.31 us

profile of v6, /device:TPU:1, one launch (start us, length us, event | category | flops | bytes accessed | tf_op | source)
XLA Modules:
  0.0 65.0 jit_solution(556647858601871409)
XLA Ops:
  0.6 61.9 %gather_grad_project.1 = (bf16[1024,512]{1,0:T(8,128)(2,1)}, f32[64,512]{1,0:T(8,128)}, bf16[2,64,512]{2,1,0:T(8,128)(2,1)}, bf16[64,512]{1,0:T(8,128)(2,1)}) custom-call(s32[32]{0:T(128)} %nown_ref.1, s32[1,32]{1,0:T(1,128)} %bitcast.2, s32[1,128]{1,0:T(1,128)} %bitcast.3, bf16[1024,8192]{1,0:T(8,128)(2,1)} %tok_hbm.1, bf16[1024,512]{1,0:T(8,128)(2,1)} %cot_hbm.1, ...), custom_call_target="tpu_custom_call" | custom-call | tf_op jit(solution)/shard_map/gather_grad_project/pallas_call | solution.py:569
  62.5 2.3 %adamw.1 = (bf16[1024,512]{1,0:T(8,128)(2,1)}, bf16[64,512]{1,0:T(8,128)(2,1)}, f32[64,512]{1,0:T(8,128)}, f32[64,512]{1,0:T(8,128)}) custom-call(bf16[1024,512]{1,0:T(8,128)(2,1)} %get-tuple-element.8.proj_hbm, f32[64,512]{1,0:T(8,128)} %get-tuple-element.9.grad_hbm, bf16[2,64,512]{2,1,0:T(8,128)(2,1)} %get-tuple-element.10.m_hbm, ...), custom_call_target="tpu_custom_call" | custom-call | tf_op jit(solution)/shard_map/adamw/pallas_call | solution.py:659
